TPU v7x, 128 devices: a whole 4x4x4 slice. The times are simulated.
128 devices in a mesh: chi: 2 (over core), phi: 64 (over z, y, x).
Axes of the slice: x: 4, y: 4, z: 4, core: 2. Of those that a mesh axis runs over, the one named last changes fastest.
Arguments:
- frames: bfloat16 [1024, 8, 8, 2048], P('phi', 'chi'), may hold values from 0.25 to 8
- drift_rows: int32 [1024, 8], P('phi', 'chi'), may hold values from -2 to 2
- drift_cols: int32 [1024, 8], P('phi', 'chi'), may hold values from -24 to 24
- weight_index: int32 [1024, 8], P('phi', 'chi'), may hold values from 0 to 63
- blur_band: int32 [16384], P('chi'), may hold values from 0 to 3
Outputs:
- restored: float32 [1024, 8, 16384], P('phi', None, 'chi')
All inputs are finite; a program needn't handle non-finite values.
Results may differ from a plain program's by a relative error of at most 0.0003.
Values sent between devices are 32-bit elements; how exact they have to be, the bound alone decides.
A program may use at most 128 MiB of HBM per device.

v0:
```python
import jax
import jax.numpy as jnp
from jax import lax
from jax.sharding import PartitionSpec as P

ITERS = 3


def shifted(shard, axis, by):
    length = lax.axis_size(axis)
    pairs = [(i, i + by) for i in range(length) if 0 <= i + by < length]
    return lax.ppermute(shard, axis, pairs)


def shift_one(frame, row_drift, col_drift, table_index):
    padded = jnp.pad(frame.astype(jnp.float32), ((3, 3), (25, 25)))
    frac_y = (table_index // 8).astype(jnp.float32) / 8.0
    frac_x = (table_index % 8).astype(jnp.float32) / 8.0
    summed = jnp.zeros(frame.shape, jnp.float32)
    for a in range(2):
        for b in range(2):
            factor = (frac_y if a else 1.0 - frac_y) * (frac_x if b else 1.0 - frac_x)
            start_row = 3 - row_drift - a
            start_col = 25 - col_drift - b
            window = lax.dynamic_slice(padded, (start_row, start_col), frame.shape)
            summed = summed + factor * window
    return summed.reshape(-1)


def tap_weights(band_index):
    spread = 0.8 + 0.6 * band_index.astype(jnp.float32)
    offsets = jnp.arange(-4, 5).astype(jnp.float32)
    unnormed = jnp.exp(-offsets[:, None] ** 2 / (2.0 * spread[None, :] ** 2))
    return unnormed / jnp.sum(unnormed, axis=0, keepdims=True)


def phi_blur(field, weights):
    number = field.shape[1]
    padded = jnp.pad(field, ((0, 0), (4, 4), (0, 0)))
    phi_sum = jnp.zeros(field.shape, jnp.float32)
    for k in range(9):
        phi_sum = phi_sum + weights[k][None, None, :] * padded[:, k : k + number, :]
    return phi_sum


def chi_mix(own, below, above):
    before = jnp.concatenate([below, own[:-1]], axis=0)
    after = jnp.concatenate([own[1:], above], axis=0)
    return 0.25 * before + 0.5 * own + 0.25 * after


def body(frames, drift_rows, drift_cols, weight_index, blur_band):
    corrected = jax.vmap(jax.vmap(shift_one))(frames, drift_rows, drift_cols, weight_index)
    pixel_tiles = lax.all_to_all(corrected, "chi", split_axis=2, concat_axis=1, tiled=True)
    weights = tap_weights(blur_band)
    estimate = pixel_tiles + 0.1
    for iteration in range(ITERS):
        summed = phi_blur(estimate, weights)
        below = shifted(summed[-1:], "phi", 1)
        above = shifted(summed[:1], "phi", -1)
        blurred = chi_mix(summed, below, above)
        ratio = pixel_tiles / (blurred + 0.1)
        ratio_sum = phi_blur(ratio, weights)
        ratio_below = shifted(ratio_sum[-1:], "phi", 1)
        ratio_above = shifted(ratio_sum[:1], "phi", -1)
        estimate = estimate * chi_mix(ratio_sum, ratio_below, ratio_above)
    return estimate


def solution(mesh):
    return jax.shard_map(
        body,
        mesh=mesh,
        in_specs=(
            P("phi", "chi", None, None),
            P("phi", "chi"),
            P("phi", "chi"),
            P("phi", "chi"),
            P("chi"),
        ),
        out_specs=P("phi", None, "chi"),
        check_vma=False,
    )
```

profile of v0, /device:TPU:97, one launch (start us, length us, event | category | flops | bytes accessed | tf_op | source)
XLA Modules:
  0.0 1749.5 jit_solution(11334240100492443829)
XLA Ops:
  0.9 8.4 pad_convert_fusion
  11.9 306.2 %while.4 = (s32[]{:T(128)}, f32[16,4,14,2098]{3,2,1,0:T(8,128)}, s32[64,4]{0,1:T(4,128)S(1)}, f32[64,8,2048]{2,1,0:T(8,128)}, s32[]{:T(128)}) while((s32[]{:T(128)}, f32[16,4,14,2098]{3,2,1,0:T(8,128)}, s32[64,4]{0,1:T(4,128)S(1)}, f32[64,8,2048]{2,1,0:T(8,128)}, s32[]{:T(128)}) %tuple.108), condition=%wide.while_cond, body=%wide.while_body.sunk | while | flops 2 | bytes 133761 | solution.py:25
  326.8 306.4 %while.5 = (s32[]{:T(128)}, f32[16,4,14,2098]{3,2,1,0:T(8,128)}, s32[64,4]{0,1:T(4,128)S(1)}, f32[64,8,2048]{2,1,0:T(8,128)}, s32[]{:T(128)}) while((s32[]{:T(128)}, f32[16,4,14,2098]{3,2,1,0:T(8,128)}, s32[64,4]{0,1:T(4,128)S(1)}, f32[64,8,2048]{2,1,0:T(8,128)}, s32[]{:T(128)}) %tuple.111), condition=%wide.while_cond.1, body=%wide.while_body.1.sunk | while | flops 2 | bytes 133761 | solution.py:25
  642.0 306.8 %while.6 = (s32[]{:T(128)}, f32[16,4,14,2098]{3,2,1,0:T(8,128)}, s32[64,4]{0,1:T(4,128)S(1)}, f32[64,8,2048]{2,1,0:T(8,128)}, s32[]{:T(128)}) while((s32[]{:T(128)}, f32[16,4,14,2098]{3,2,1,0:T(8,128)}, s32[64,4]{0,1:T(4,128)S(1)}, f32[64,8,2048]{2,1,0:T(8,128)}, s32[]{:T(128)}) %tuple.112), condition=%wide.while_cond.2, body=%wide.while_body.2.sunk | while | flops 2 | bytes 133761 | solution.py:25
  957.5 303.8 %while.7 = (s32[]{:T(128)}, f32[16,4,14,2098]{3,2,1,0:T(8,128)}, s32[64,4]{0,1:T(4,128)S(1)}, f32[64,8,2048]{2,1,0:T(8,128)}, s32[]{:T(128)}) while((s32[]{:T(128)}, f32[16,4,14,2098]{3,2,1,0:T(8,128)}, s32[64,4]{0,1:T(4,128)S(1)}, f32[64,8,2048]{2,1,0:T(8,128)}, s32[]{:T(128)}) %tuple.113), condition=%wide.while_cond.3, body=%wide.while_body.3.sunk | while | flops 2 | bytes 133761 | solution.py:25
  1267.7 8.6 multiply_add_fusion
  1276.3 23.6 %copy.59 = f32[16,4,16384]{0,1,2:T(4,128)} copy(f32[16,4,16384]{2,1,0:T(4,128)} %multiply_add_fusion) | data formatting | bytes 8388608 | tf_op jit(solution)/shard_map/vmap(vmap())/add | solution.py:26
  1299.9 42.6 %reshape.139 = f32[2,1,524288]{2,1,0:T(1,128)} reshape(f32[16384,4,16]{2,1,0:T(4,128)} %bitcast.94) | data formatting | bytes 8388608
  1353.4 16.7 reduce
  1370.1 44.6 %reshape.140 = f32[16384,4,16]{2,1,0:T(4,128)} reshape(f32[2,524288]{1,0:T(2,128)} %reduce) | data formatting | bytes 8388608
  1414.8 25.1 %copy.60 = f32[16,2,4,8192]{3,2,1,0:T(4,128)} copy(f32[16,2,4,8192]{0,2,3,1:T(4,128)} %bitcast.95) | data formatting | bytes 8388608 | tf_op jit(solution)/shard_map/all_to_all | solution.py:54
  1467.6 21.8 %fusion.99 = f32[16,8,8192]{2,1,0:T(8,128)} fusion(f32[16,8,8192]{2,1,0:T(8,128)} %all_to_all.16, f32[15,8,8192]{2,1,0:T(8,128)} %get-tuple-element.108, f32[1,8,8192]{2,1,0:T(8,128)S(1)} %collective-permute-done, f32[1,8,8192]{2,1,0:T(8,128)S(1)} %collective-permute-done.1, f32[15,8,8192]{2,1,0:T(8,128)} %get-tuple-element.107, f32[8192]{0:T(1024)S(1)} %bitcast.109, ...), kind=kLoop, calls=%fused_computation.157 | loop fusion | flops 27262976 | bytes 21266432 | tf_op jit(solution)/shard_map/div | solution.py:62
  1489.4 16.1 fusion.24
  1507.5 8.5 collective-permute-start.3
  1520.0 21.3 %fusion.102 = f32[16,8,8192]{2,1,0:T(8,128)} fusion(f32[15,8,8192]{2,1,0:T(8,128)} %get-tuple-element.104, f32[1,8,8192]{2,1,0:T(8,128)S(1)} %collective-permute-done.2, f32[1,8,8192]{2,1,0:T(8,128)S(1)} %collective-permute-done.3, f32[15,8,8192]{2,1,0:T(8,128)} %get-tuple-element.103, f32[16,8,8192]{2,1,0:T(8,128)} %all_to_all.16, f32[8192]{0:T(1024)S(1)} %bitcast.111, ...), kind=kLoop, calls=%fused_computation.162 | loop fusion | flops 27262976 | bytes 21266432 | tf_op jit(solution)/shard_map/mul | solution.py:66
  1541.2 16.6 fusion.40
  1559.9 8.5 collective-permute-start.5
  1572.3 21.8 %fusion.106 = f32[16,8,8192]{2,1,0:T(8,128)} fusion(f32[16,8,8192]{2,1,0:T(8,128)} %all_to_all.16, f32[15,8,8192]{2,1,0:T(8,128)} %get-tuple-element.100, f32[1,8,8192]{2,1,0:T(8,128)S(1)} %collective-permute-done.4, f32[1,8,8192]{2,1,0:T(8,128)S(1)} %collective-permute-done.5, f32[15,8,8192]{2,1,0:T(8,128)} %get-tuple-element.99, f32[8192]{0:T(1024)S(1)} %bitcast.113, ...), kind=kLoop, calls=%fused_computation.168 | loop fusion | flops 27262976 | bytes 21266432 | tf_op jit(solution)/shard_map/div | solution.py:62
  1594.1 16.1 fusion.56
  1624.0 21.3 %fusion.109 = f32[16,8,8192]{2,1,0:T(8,128)} fusion(f32[16,8,8192]{2,1,0:T(8,128)} %fusion.102, f32[15,8,8192]{2,1,0:T(8,128)} %get-tuple-element.96, f32[1,8,8192]{2,1,0:T(8,128)S(1)} %collective-permute-done.6, f32[1,8,8192]{2,1,0:T(8,128)S(1)} %collective-permute-done.7, f32[15,8,8192]{2,1,0:T(8,128)} %get-tuple-element.95, f32[8192]{0:T(1024)S(1)} %bitcast.115, ...), kind=kLoop, calls=%fused_computation.173 | loop fusion | flops 26214400 | bytes 21266432 | tf_op jit(solution)/shard_map/mul | solution.py:66
  1645.3 16.6 fusion.72
  1675.8 21.8 %fusion.113 = f32[16,8,8192]{2,1,0:T(8,128)} fusion(f32[16,8,8192]{2,1,0:T(8,128)} %all_to_all.16, f32[15,8,8192]{2,1,0:T(8,128)} %get-tuple-element.92, f32[1,8,8192]{2,1,0:T(8,128)S(1)} %collective-permute-done.8, f32[1,8,8192]{2,1,0:T(8,128)S(1)} %collective-permute-done.9, f32[15,8,8192]{2,1,0:T(8,128)} %get-tuple-element.91, f32[8192]{0:T(1024)S(1)} %bitcast.117, ...), kind=kLoop, calls=%fused_computation.179 | loop fusion | flops 27262976 | bytes 21266432 | tf_op jit(solution)/shard_map/div | solution.py:62
  1697.6 16.3 fusion.88
  1727.6 21.5 %fusion.116 = f32[16,8,8192]{2,1,0:T(8,128)} fusion(f32[16,8,8192]{2,1,0:T(8,128)} %fusion.109, f32[15,8,8192]{2,1,0:T(8,128)} %get-tuple-element.88, f32[1,8,8192]{2,1,0:T(8,128)S(1)} %collective-permute-done.10, f32[1,8,8192]{2,1,0:T(8,128)S(1)} %collective-permute-done.11, f32[15,8,8192]{2,1,0:T(8,128)} %get-tuple-element.87, f32[8192]{0:T(1024)S(1)} %bitcast.119, ...), kind=kLoop, calls=%fused_computation.184 | loop fusion | flops 26214400 | bytes 21266432 | tf_op jit(solution)/shard_map/mul | solution.py:66
  (845 shorter events, 1350.3 us)
Async XLA Ops:
  1261.3 6.0 copy-start.2
  1342.5 10.4 all-to-all-start
  1445.1 2.6 copy-start.1
  1447.7 5.3 copy-start
  1453.1 13.6 collective-permute-start
  1456.2 11.4 collective-permute-start.1
  1505.6 14.4 collective-permute-start.2
  1507.5 12.5 collective-permute-start.3
  1557.9 14.4 collective-permute-start.4
  1559.9 12.4 collective-permute-start.5
  1610.3 13.7 collective-permute-start.6
  1612.2 11.8 collective-permute-start.7
  1662.0 13.8 collective-permute-start.8
  1663.9 11.9 collective-permute-start.9
  1714.0 13.5 collective-permute-start.10
  1716.0 11.6 collective-permute-start.11
where the time goes:
time: 1780 us; the launch traced here: 1750 us
  local copies, waits for them, and re-layouts  1420 us (80%)
  other arithmetic  254 us (14%)
  starting transfers between devices  65.6 us (4%)
    gather x768, local copies, waits for them, and re-layouts  1220 us
    unnamed x14, local copies, waits for them, and re-layouts  97.3 us
    add x6, other arithmetic, phi_blur(): phi_sum = phi_sum + weights[k][None, None, :] * padded[:, k:k + number, :]  86.5 us
    div x3, other arithmetic, body(): ratio = pixel_tiles / (blurred + 0.1)  65.5 us
    mul x3, other arithmetic, body(): estimate = estimate * chi_mix(ratio_sum, ratio_below, ratio_above)  64.1 us
    ppermute x12, starting transfers between devices, shifted(): return lax.ppermute(shard, axis, pairs)  59.4 us
  transfers between devices with their start and end apart: 13, of which 3 were waited for; matrix products, arithmetic and copies ran while one was open for 1% of the time, Pallas kernels for 0%

commit v1 on v0

v1 whole, which is shorter than its diff:
```python
import functools

import jax
import jax.numpy as jnp
from jax import lax
from jax.experimental import pallas as pl
from jax.experimental.pallas import tpu as pltpu
from jax.sharding import PartitionSpec as P

ITERS = 3
HALO = 2 * ITERS
LANES = 128
SUBS = 8
PAD_ROWS = 3
REMOTE = 4


def shift_tilt(tilt, rows_ref, cols_ref, index_ref, frames_ref, spread_ref, staged_ref):
    own_phis, rows, cols = frames_ref.shape[1:]
    tiles = cols // LANES
    halves = tiles // SUBS
    blocks = staged_ref.shape[1]
    lane = lax.broadcasted_iota(jnp.int32, (rows, LANES), 1)
    zero = jnp.zeros((rows, LANES), jnp.float32)
    for p in range(own_phis):
        drift_col = cols_ref[tilt, p]
        frac_x = (index_ref[tilt, p] & 7).astype(jnp.float32) / 8.0
        turn = (drift_col + LANES) & (LANES - 1)
        from_left = lane < drift_col
        from_right = lane >= LANES + drift_col
        frame = frames_ref[tilt, p].astype(jnp.float32)
        source = [frame[:, t * LANES : (t + 1) * LANES] for t in range(tiles)] + [zero]
        stepped = [pltpu.roll(s, 1, 1) for s in source[:-1]]
        turned = []
        for t in range(tiles + 1):
            before = stepped[t - 1] if t > 0 else zero
            here = stepped[t] if t < tiles else zero
            mixed = (1.0 - frac_x) * source[t] + frac_x * jnp.where(lane < 1, before, here)
            turned.append(pltpu.roll(mixed, turn, 1))
        moved = []
        for t in range(tiles):
            left = turned[t - 1] if t > 0 else zero
            moved.append(jnp.where(from_left, left, jnp.where(from_right, turned[t + 1], turned[t])))
        for h in range(halves):
            group = jnp.stack(moved[h * SUBS : (h + 1) * SUBS])
            spread_ref[p, PAD_ROWS : PAD_ROWS + rows, h] = jnp.swapaxes(group, 0, 1)
    for p in range(own_phis):
        drift_row = rows_ref[tilt, p]
        frac_y = (index_ref[tilt, p] >> 3).astype(jnp.float32) / 8.0
        for r in range(rows):
            row = (1.0 - frac_y) * spread_ref[p, r + PAD_ROWS - drift_row] + frac_y * spread_ref[
                p, r + PAD_ROWS - 1 - drift_row
            ]
            for h in range(halves):
                place = r * halves + h
                staged_ref[place // blocks, place % blocks, tilt, p] = row[h]


def tap_matrices(band):
    spread = 0.8 + 0.6 * band.astype(jnp.float32)
    unnormed = [jnp.exp(-float(k * k) / (2.0 * spread * spread)) for k in range(5)]
    total = unnormed[0] + 2.0 * (unnormed[1] + unnormed[2] + unnormed[3] + unnormed[4])
    taps = [0.125 * (u / total) for u in unnormed]
    made = {}

    def pair(near, far, sign):
        if far > 4:
            return taps[near]
        if (near, far, sign) not in made:
            made[near, far, sign] = taps[near] + sign * taps[far] if near < far else taps[near] * 1.0 + sign * taps[far]
        return made[near, far, sign]

    even = [[pair(abs(p - q), 7 - p - q, 1.0) for q in range(4)] for p in range(4)]
    odd = [[pair(abs(p - q), 7 - p - q, -1.0) for q in range(4)] for p in range(4)]
    return even, odd


def phi_blur(tilts, even, odd):
    plus = [tilts[p] + tilts[7 - p] for p in range(4)]
    minus = [tilts[p] - tilts[7 - p] for p in range(4)]
    halves = []
    for matrix, parts in ((even, plus), (odd, minus)):
        rows = []
        for p in range(4):
            row = matrix[p][0] * parts[0]
            for q in range(1, 4):
                row = row + matrix[p][q] * parts[q]
            rows.append(row)
        halves.append(rows)
    front = [halves[0][p] + halves[1][p] for p in range(4)]
    back = [halves[0][3 - p] - halves[1][3 - p] for p in range(4)]
    return front + back


def sweep(load, emit, low, high, even, odd):
    before = phi_blur(load(low - 1), even, odd)
    here = phi_blur(load(low), even, odd)
    joined = [a + b for a, b in zip(before, here)]

    def step(c, carry):
        here, joined = carry
        after = phi_blur(load(c + 1), even, odd)
        ahead = [a + b for a, b in zip(here, after)]
        emit(c, [a + b for a, b in zip(joined, ahead)])
        return after, ahead

    lax.fori_loop(low, high, step, (here, joined), unroll=2)


def kernel(
    n_phi,
    rows_ref,
    cols_ref,
    index_ref,
    band_ref,
    frames_hbm,
    out_hbm,
    frames_ref,
    spread_ref,
    staged_ref,
    data_ref,
    estimate_ref,
    ratio_ref,
    done_ref,
    frame_sems,
    send_sems,
    recv_sems,
    pair_sends,
    pair_recvs,
    local_sems,
    out_sems,
):
    chi, phi = lax.axis_index("chi"), lax.axis_index("phi")
    other = 1 - chi
    before = lax.rem(phi + n_phi - 1, n_phi)
    after = lax.rem(phi + 1, n_phi)
    own_tilts, own_phis = frames_ref.shape[:2]
    blocks, all_tilts, phis = data_ref.shape[:3]
    sizes = (HALO, HALO, own_tilts - 2 * HALO)
    firsts = (0, own_tilts - HALO, HALO)

    loads = []
    for number, (first, size) in enumerate(zip(firsts, sizes)):
        part = pl.ds(first, size)
        loads.append(pltpu.make_async_copy(frames_hbm.at[part], frames_ref.at[part], frame_sems.at[number]))
        loads[-1].start()

    barrier = pltpu.get_barrier_semaphore()
    peers = [(before, 0), (before, 1), (after, 0), (after, 1)]
    for to_phi, to_chi in peers + [(phi, other)]:
        pl.semaphore_signal(
            barrier, inc=1, device_id={"chi": to_chi, "phi": to_phi}, device_id_type=pl.DeviceIdType.MESH
        )

    empty = jnp.zeros(spread_ref.shape[2:], jnp.float32)
    for p in range(own_phis):
        for r in range(PAD_ROWS):
            spread_ref[p, r] = empty
            spread_ref[p, spread_ref.shape[1] - 1 - r] = empty

    def shift_tilts(first, size):
        def step(tilt, carry):
            shift_tilt(tilt, rows_ref, cols_ref, index_ref, frames_ref, spread_ref, staged_ref)
            return carry

        lax.fori_loop(first, first + size, step, 0)

    mine = pl.ds(chi * own_phis, own_phis)

    def neighbour_copy(b, number):
        to_phi, to_chi = peers[number]
        back = number < 2
        from_tilts = pl.ds(0 if back else own_tilts - HALO, HALO)
        to_tilts = pl.ds(all_tilts - HALO if back else 0, HALO)
        place = (0 if back else 2) + chi
        return pltpu.make_async_remote_copy(
            src_ref=staged_ref.at[to_chi, b, from_tilts],
            dst_ref=data_ref.at[b, to_tilts, mine],
            send_sem=send_sems.at[b, number],
            recv_sem=recv_sems.at[b, place],
            device_id={"chi": to_chi, "phi": to_phi},
            device_id_type=pl.DeviceIdType.MESH,
        )

    def arrival(b, place):
        back = place < 2
        to_tilts = pl.ds(all_tilts - HALO if back else 0, HALO)
        from_chi = place % 2
        return pltpu.make_async_remote_copy(
            src_ref=staged_ref.at[0, b, pl.ds(0, HALO)],
            dst_ref=data_ref.at[b, to_tilts, pl.ds(from_chi * own_phis, own_phis)],
            send_sem=send_sems.at[b, place],
            recv_sem=recv_sems.at[b, place],
            device_id={"chi": from_chi, "phi": after if back else before},
            device_id_type=pl.DeviceIdType.MESH,
        )

    middle = pl.ds(HALO, own_tilts)

    def pair_copy(b, phis_at):
        return pltpu.make_async_remote_copy(
            src_ref=staged_ref.at[other, b],
            dst_ref=data_ref.at[b, middle, phis_at],
            send_sem=pair_sends.at[b],
            recv_sem=pair_recvs.at[b],
            device_id={"chi": other, "phi": phi},
            device_id_type=pl.DeviceIdType.MESH,
        )

    def local_copy(b):
        return pltpu.make_async_copy(staged_ref.at[chi, b], data_ref.at[b, middle, mine], local_sems.at[b])

    loads[0].wait()
    shift_tilts(firsts[0], sizes[0])
    loads[1].wait()
    shift_tilts(firsts[1], sizes[1])
    pl.semaphore_wait(barrier, len(peers) + 1)

    def send_halos(b, carry):
        for number in range(REMOTE):
            neighbour_copy(b, number).start()
        return carry

    lax.fori_loop(0, blocks, send_halos, 0)
    loads[2].wait()
    shift_tilts(firsts[2], sizes[2])

    def send_pairs(b, carry):
        pair_copy(b, mine).start()
        local_copy(b).start()
        return carry

    lax.fori_loop(0, blocks, send_pairs, 0)

    left_add = jnp.where(phi == 0, 0.0, 0.1)
    right_add = jnp.where(phi == n_phi - 1, 0.0, 0.1)

    def out_copy(b, p):
        return pltpu.make_async_copy(
            done_ref.at[b, :, p], out_hbm.at[:, pl.ds(b * SUBS, SUBS), p, :], out_sems.at[b, p]
        )

    def block(b, carry):
        for place in range(REMOTE):
            arrival(b, place).wait_recv()
        pair_copy(b, pl.ds(other * own_phis, own_phis)).wait_recv()
        local_copy(b).wait()
        nothing = jnp.zeros((HALO,) + data_ref.shape[2:], jnp.float32)

        @pl.when(phi == 0)
        def _():
            data_ref[b, 0:HALO] = nothing

        @pl.when(phi == n_phi - 1)
        def _():
            data_ref[b, all_tilts - HALO : all_tilts] = nothing

        even, odd = tap_matrices(band_ref[pl.ds(pl.multiple_of(b * SUBS, SUBS), SUBS), :])

        def start(c):
            add = jnp.where(c < HALO, left_add, jnp.where(c >= HALO + own_tilts, right_add, 0.1))
            return [data_ref[b, c, p] + add for p in range(phis)]

        def held(c):
            return [estimate_ref[c, p] for p in range(phis)]

        def ratios(c):
            return [ratio_ref[c, p] for p in range(phis)]

        for iteration in range(ITERS):
            estimate = start if iteration == 0 else held
            margin = 2 * iteration + 1

            def to_ratio(c, blurred):
                for p in range(phis):
                    ratio_ref[c, p] = data_ref[b, c, p] / (blurred[p] + 0.1)

            def to_estimate(c, factor):
                old = estimate(c)
                for p in range(phis):
                    if iteration == ITERS - 1:
                        done_ref[b, c - HALO, p] = old[p] * factor[p]
                    else:
                        estimate_ref[c, p] = old[p] * factor[p]

            sweep(estimate, to_ratio, margin, all_tilts - margin, even, odd)
            sweep(ratios, to_estimate, margin + 1, all_tilts - margin - 1, even, odd)
        for p in range(phis):
            out_copy(b, p).start()
        return carry

    lax.fori_loop(0, blocks, block, 0)

    def finish(b, carry):
        for number in range(REMOTE):
            neighbour_copy(b, number).wait_send()
        pair_copy(b, mine).wait_send()
        for p in range(phis):
            out_copy(b, p).wait()
        return carry

    lax.fori_loop(0, blocks, finish, 0)


def body(n_phi, frames, drift_rows, drift_cols, weight_index, blur_band):
    tilts, own_phis, rows, cols = frames.shape
    pixels = blur_band.shape[0]
    phis = 2 * own_phis
    planes = pixels // LANES
    blocks = planes // SUBS
    tile = (SUBS, LANES)
    all_tilts = tilts + 2 * HALO
    smem = pl.BlockSpec(memory_space=pltpu.SMEM)
    vmem = pl.BlockSpec(memory_space=pltpu.VMEM)
    out = pl.pallas_call(
        functools.partial(kernel, n_phi),
        out_shape=jax.ShapeDtypeStruct((tilts, planes, phis, LANES), jnp.float32),
        in_specs=[smem, smem, smem, vmem, pl.BlockSpec(memory_space=pl.ANY)],
        out_specs=pl.BlockSpec(memory_space=pl.ANY),
        scratch_shapes=[
            pltpu.VMEM(frames.shape, frames.dtype),
            pltpu.VMEM((own_phis, rows + 2 * PAD_ROWS, cols // LANES // SUBS) + tile, jnp.float32),
            pltpu.VMEM((2, blocks, tilts, own_phis) + tile, jnp.float32),
            pltpu.VMEM((blocks, all_tilts, phis) + tile, jnp.float32),
            pltpu.VMEM((all_tilts, phis) + tile, jnp.float32),
            pltpu.VMEM((all_tilts, phis) + tile, jnp.float32),
            pltpu.VMEM((blocks, tilts, phis) + tile, jnp.float32),
            pltpu.SemaphoreType.DMA((3,)),
            pltpu.SemaphoreType.DMA((blocks, REMOTE)),
            pltpu.SemaphoreType.DMA((blocks, REMOTE)),
            pltpu.SemaphoreType.DMA((blocks,)),
            pltpu.SemaphoreType.DMA((blocks,)),
            pltpu.SemaphoreType.DMA((blocks,)),
            pltpu.SemaphoreType.DMA((blocks, phis)),
        ],
        compiler_params=pltpu.CompilerParams(
            collective_id=0, has_side_effects=True, vmem_limit_bytes=48 * 1024 * 1024
        ),
        name="rocking",
    )(drift_rows, drift_cols, weight_index, blur_band.reshape(planes, LANES), frames)
    return out.transpose(0, 2, 1, 3).reshape(tilts, phis, pixels)


def solution(mesh):
    return jax.shard_map(
        functools.partial(body, mesh.shape["phi"]),
        mesh=mesh,
        in_specs=(
            P("phi", "chi", None, None),
            P("phi", "chi"),
            P("phi", "chi"),
            P("phi", "chi"),
            P("chi"),
        ),
        out_specs=P("phi", None, "chi"),
        check_vma=False,
    )
```

time: 1780 us -> 62.6 us (0.04)
  the two profiles are of different devices: /device:TPU:97 before, /device:TPU:1 now
where the time goes in v1:
time: 62.6 us; the launch traced here: 62.3 us
  Pallas kernels  53 us (85%)
  local copies, waits for them, and re-layouts  9.23 us (15%)
    pallas_call x1, Pallas kernels, body(): pl.pallas_call(functools.partial(kernel, n_phi), out_shape=jax.ShapeDtype...  53 us
    unnamed x8, local copies, waits for them, and re-layouts  9.23 us

profile of v1, /device:TPU:1, one launch (start us, length us, event | category | flops | bytes accessed | tf_op | source)
XLA Modules:
  0.0 62.3 jit_solution(13763550920989919554)
XLA Ops:
  0.0 0.8 %copy.6.rows_ref = s32[16,4]{1,0:T(8,128)S(1)} copy(s32[16,4]{0,1:T(4,128)} %param.6) | data formatting | bytes 512 | tf_op args[1]
  0.8 0.8 %copy.7.cols_ref = s32[16,4]{1,0:T(8,128)S(1)} copy(s32[16,4]{0,1:T(4,128)} %param.7) | data formatting | bytes 512 | tf_op args[2]
  1.5 0.8 %copy.8.index_ref = s32[16,4]{1,0:T(8,128)S(1)} copy(s32[16,4]{0,1:T(4,128)} %param.8) | data formatting | bytes 512 | tf_op args[3]
  2.3 0.0 copy-start
  2.3 1.6 %copy-done = bf16[16,4,8,2048]{3,2,1,0:T(8,128)(2,1)S(1)} copy-done((bf16[16,4,8,2048]{3,2,1,0:T(8,128)(2,1)S(1)}, bf16[16,4,8,2048]{3,2,1,0:T(8,128)(2,1)}, u32[]{:S(2)}) %copy-start) | copy-done | bytes 2097176
  3.9 0.0 copy-start.1
  3.9 0.8 %copy-done.1 = s32[8192]{0:T(1024)S(1)} copy-done((s32[8192]{0:T(1024)S(1)}, s32[8192]{0:T(1024)}, u32[]{:S(2)}) %copy-start.1) | copy-done | bytes 32792
  4.6 53.0 %rocking.1 = f32[16,64,8,128]{3,2,1,0:T(8,128)} custom-call(s32[16,4]{1,0:T(8,128)S(1)} %copy.6.rows_ref, s32[16,4]{1,0:T(8,128)S(1)} %copy.7.cols_ref, s32[16,4]{1,0:T(8,128)S(1)} %copy.8.index_ref, s32[64,128]{1,0:T(8,128)S(1)} %bitcast.4, bf16[16,4,8,2048]{3,2,1,0:T(8,128)(2,1)S(1)} %copy-done), custom_call_target="tpu_custom_call" | custom-call | tf_op jit(solution)/shard_map/rocking/pallas_call | solution.py:315
  57.7 4.6 %copy.10 = f32[16,8,8192]{2,1,0:T(8,128)} copy(f32[16,8,8192]{2,1,0:T(8,128)} %bitcast.5) | data formatting | bytes 8388608
Async XLA Ops:
  2.3 1.6 %copy-start = (bf16[16,4,8,2048]{3,2,1,0:T(8,128)(2,1)S(1)}, bf16[16,4,8,2048]{3,2,1,0:T(8,128)(2,1)}, u32[]{:S(2)}) copy-start(bf16[16,4,8,2048]{3,2,1,0:T(8,128)(2,1)} %frames_hbm.1) | copy-start | bytes 6291460
  3.9 0.8 %copy-start.1 = (s32[8192]{0:T(1024)S(1)}, s32[8192]{0:T(1024)}, u32[]{:S(2)}) copy-start(s32[8192]{0:T(1024)} %param.9) | copy-start | bytes 98308

commit v2 on v1

--- a/solution.py
+++ b/solution.py
@@ -11,7 +11,8 @@
 HALO = 2 * ITERS
 LANES = 128
 SUBS = 8
-PAD_ROWS = 3
+MOST_ROWS = 2
+PAD_ROWS = MOST_ROWS + 1
 REMOTE = 4
 
 
@@ -23,8 +24,8 @@
     lane = lax.broadcasted_iota(jnp.int32, (rows, LANES), 1)
     zero = jnp.zeros((rows, LANES), jnp.float32)
     for p in range(own_phis):
-        drift_col = cols_ref[tilt, p]
-        frac_x = (index_ref[tilt, p] & 7).astype(jnp.float32) / 8.0
+        drift_col = cols_ref[p, tilt]
+        frac_x = (index_ref[p, tilt] & 7).astype(jnp.float32) / 8.0
         turn = (drift_col + LANES) & (LANES - 1)
         from_left = lane < drift_col
         from_right = lane >= LANES + drift_col
@@ -45,8 +46,8 @@
             group = jnp.stack(moved[h * SUBS : (h + 1) * SUBS])
             spread_ref[p, PAD_ROWS : PAD_ROWS + rows, h] = jnp.swapaxes(group, 0, 1)
     for p in range(own_phis):
-        drift_row = rows_ref[tilt, p]
-        frac_y = (index_ref[tilt, p] >> 3).astype(jnp.float32) / 8.0
+        drift_row = rows_ref[p, tilt]
+        frac_y = (index_ref[p, tilt] >> 3).astype(jnp.float32) / 8.0
         for r in range(rows):
             row = (1.0 - frac_y) * spread_ref[p, r + PAD_ROWS - drift_row] + frac_y * spread_ref[
                 p, r + PAD_ROWS - 1 - drift_row
@@ -112,33 +113,36 @@
     rows_ref,
     cols_ref,
     index_ref,
+    band_hbm,
+    frames_hbm,
+    out_ref,
     band_ref,
-    frames_hbm,
-    out_hbm,
     frames_ref,
     spread_ref,
     staged_ref,
     data_ref,
     estimate_ref,
     ratio_ref,
-    done_ref,
+    band_sem,
     frame_sems,
     send_sems,
     recv_sems,
     pair_sends,
     pair_recvs,
     local_sems,
-    out_sems,
 ):
     chi, phi = lax.axis_index("chi"), lax.axis_index("phi")
     other = 1 - chi
     before = lax.rem(phi + n_phi - 1, n_phi)
     after = lax.rem(phi + 1, n_phi)
+    has_before, has_after = phi > 0, phi < n_phi - 1
     own_tilts, own_phis = frames_ref.shape[:2]
     blocks, all_tilts, phis = data_ref.shape[:3]
     sizes = (HALO, HALO, own_tilts - 2 * HALO)
     firsts = (0, own_tilts - HALO, HALO)
 
+    band_load = pltpu.make_async_copy(band_hbm, band_ref, band_sem)
+    band_load.start()
     loads = []
     for number, (first, size) in enumerate(zip(firsts, sizes)):
         part = pl.ds(first, size)
@@ -147,10 +151,25 @@
 
     barrier = pltpu.get_barrier_semaphore()
     peers = [(before, 0), (before, 1), (after, 0), (after, 1)]
-    for to_phi, to_chi in peers + [(phi, other)]:
+
+    def greet(to_phi, to_chi):
         pl.semaphore_signal(
             barrier, inc=1, device_id={"chi": to_chi, "phi": to_phi}, device_id_type=pl.DeviceIdType.MESH
         )
+
+    def with_neighbours(act):
+        @pl.when(has_before)
+        def _():
+            for number in (0, 1):
+                act(number)
+
+        @pl.when(has_after)
+        def _():
+            for number in (2, 3):
+                act(number)
+
+    with_neighbours(lambda number: greet(*peers[number]))
+    greet(phi, other)
 
     empty = jnp.zeros(spread_ref.shape[2:], jnp.float32)
     for p in range(own_phis):
@@ -214,11 +233,10 @@
     shift_tilts(firsts[0], sizes[0])
     loads[1].wait()
     shift_tilts(firsts[1], sizes[1])
-    pl.semaphore_wait(barrier, len(peers) + 1)
+    pl.semaphore_wait(barrier, 1 + 2 * has_before.astype(jnp.int32) + 2 * has_after.astype(jnp.int32))
 
     def send_halos(b, carry):
-        for number in range(REMOTE):
-            neighbour_copy(b, number).start()
+        with_neighbours(lambda number: neighbour_copy(b, number).start())
         return carry
 
     lax.fori_loop(0, blocks, send_halos, 0)
@@ -231,29 +249,35 @@
         return carry
 
     lax.fori_loop(0, blocks, send_pairs, 0)
+    band_load.wait()
 
     left_add = jnp.where(phi == 0, 0.0, 0.1)
     right_add = jnp.where(phi == n_phi - 1, 0.0, 0.1)
 
-    def out_copy(b, p):
-        return pltpu.make_async_copy(
-            done_ref.at[b, :, p], out_hbm.at[:, pl.ds(b * SUBS, SUBS), p, :], out_sems.at[b, p]
-        )
-
     def block(b, carry):
-        for place in range(REMOTE):
-            arrival(b, place).wait_recv()
         pair_copy(b, pl.ds(other * own_phis, own_phis)).wait_recv()
         local_copy(b).wait()
-        nothing = jnp.zeros((HALO,) + data_ref.shape[2:], jnp.float32)
+        nothing = jnp.zeros(data_ref.shape[2:], jnp.float32)
+
+        @pl.when(has_before)
+        def _():
+            for place in (2, 3):
+                arrival(b, place).wait_recv()
 
         @pl.when(phi == 0)
         def _():
-            data_ref[b, 0:HALO] = nothing
+            for c in range(HALO):
+                data_ref[b, c] = nothing
+
+        @pl.when(has_after)
+        def _():
+            for place in (0, 1):
+                arrival(b, place).wait_recv()
 
         @pl.when(phi == n_phi - 1)
         def _():
-            data_ref[b, all_tilts - HALO : all_tilts] = nothing
+            for c in range(all_tilts - HALO, all_tilts):
+                data_ref[b, c] = nothing
 
         even, odd = tap_matrices(band_ref[pl.ds(pl.multiple_of(b * SUBS, SUBS), SUBS), :])
 
@@ -276,27 +300,23 @@
                     ratio_ref[c, p] = data_ref[b, c, p] / (blurred[p] + 0.1)
 
             def to_estimate(c, factor):
-                old = estimate(c)
-                for p in range(phis):
-                    if iteration == ITERS - 1:
-                        done_ref[b, c - HALO, p] = old[p] * factor[p]
-                    else:
-                        estimate_ref[c, p] = old[p] * factor[p]
+                made = [a * f for a, f in zip(estimate(c), factor)]
+                if iteration < ITERS - 1:
+                    for p in range(phis):
+                        estimate_ref[c, p] = made[p]
+                else:
+                    planes = pl.ds(pl.multiple_of(b * SUBS, SUBS), SUBS)
+                    out_ref[c - HALO, planes] = jnp.swapaxes(jnp.stack(made), 0, 1)
 
             sweep(estimate, to_ratio, margin, all_tilts - margin, even, odd)
             sweep(ratios, to_estimate, margin + 1, all_tilts - margin - 1, even, odd)
-        for p in range(phis):
-            out_copy(b, p).start()
         return carry
 
     lax.fori_loop(0, blocks, block, 0)
 
     def finish(b, carry):
-        for number in range(REMOTE):
-            neighbour_copy(b, number).wait_send()
+        with_neighbours(lambda number: neighbour_copy(b, number).wait_send())
         pair_copy(b, mine).wait_send()
-        for p in range(phis):
-            out_copy(b, p).wait()
         return carry
 
     lax.fori_loop(0, blocks, finish, 0)
@@ -310,34 +330,34 @@
     blocks = planes // SUBS
     tile = (SUBS, LANES)
     all_tilts = tilts + 2 * HALO
+    hbm = pl.BlockSpec(memory_space=pltpu.HBM)
     smem = pl.BlockSpec(memory_space=pltpu.SMEM)
-    vmem = pl.BlockSpec(memory_space=pltpu.VMEM)
     out = pl.pallas_call(
         functools.partial(kernel, n_phi),
-        out_shape=jax.ShapeDtypeStruct((tilts, planes, phis, LANES), jnp.float32),
-        in_specs=[smem, smem, smem, vmem, pl.BlockSpec(memory_space=pl.ANY)],
-        out_specs=pl.BlockSpec(memory_space=pl.ANY),
+        out_shape=pltpu.VMEM((tilts, planes, phis, LANES), jnp.float32),
+        in_specs=[smem] * 3 + [hbm] * 2,
+        out_specs=pl.BlockSpec(memory_space=pltpu.VMEM),
         scratch_shapes=[
+            pltpu.VMEM((planes, LANES), jnp.int32),
             pltpu.VMEM(frames.shape, frames.dtype),
             pltpu.VMEM((own_phis, rows + 2 * PAD_ROWS, cols // LANES // SUBS) + tile, jnp.float32),
             pltpu.VMEM((2, blocks, tilts, own_phis) + tile, jnp.float32),
             pltpu.VMEM((blocks, all_tilts, phis) + tile, jnp.float32),
             pltpu.VMEM((all_tilts, phis) + tile, jnp.float32),
             pltpu.VMEM((all_tilts, phis) + tile, jnp.float32),
-            pltpu.VMEM((blocks, tilts, phis) + tile, jnp.float32),
+            pltpu.SemaphoreType.DMA,
             pltpu.SemaphoreType.DMA((3,)),
             pltpu.SemaphoreType.DMA((blocks, REMOTE)),
             pltpu.SemaphoreType.DMA((blocks, REMOTE)),
             pltpu.SemaphoreType.DMA((blocks,)),
             pltpu.SemaphoreType.DMA((blocks,)),
             pltpu.SemaphoreType.DMA((blocks,)),
-            pltpu.SemaphoreType.DMA((blocks, phis)),
         ],
         compiler_params=pltpu.CompilerParams(
-            collective_id=0, has_side_effects=True, vmem_limit_bytes=48 * 1024 * 1024
+            collective_id=0, has_side_effects=True, vmem_limit_bytes=56 * 1024 * 1024
         ),
         name="rocking",
-    )(drift_rows, drift_cols, weight_index, blur_band.reshape(planes, LANES), frames)
+    )(drift_rows.T, drift_cols.T, weight_index.T, blur_band.reshape(planes, LANES), frames)
     return out.transpose(0, 2, 1, 3).reshape(tilts, phis, pixels)
 
 

time: 62.6 us -> 50.3 us (0.80)
  the two profiles are of different devices: /device:TPU:1 before, /device:TPU:97 now
where the time goes in v2:
time: 50.3 us; the launch traced here: 50.1 us
  Pallas kernels  48.1 us (96%)
  local copies, waits for them, and re-layouts  2.02 us (4%)
    pallas_call x1, Pallas kernels, body(): pl.pallas_call(functools.partial(kernel, n_phi), out_shape=pltpu.VMEM((ti...  48.1 us
    unnamed x1, local copies, waits for them, and re-layouts  2.02 us

profile of v2, /device:TPU:97, one launch (start us, length us, event | category | flops | bytes accessed | tf_op | source)
XLA Modules:
  0.0 50.1 jit_solution(11952596450177951257)
XLA Ops:
  0.0 48.1 %rocking.1 = f32[16,64,8,128]{3,2,1,0:T(8,128)S(1)} custom-call(s32[4,16]{1,0:T(4,128)} %bitcast.9, s32[4,16]{1,0:T(4,128)} %bitcast.10, s32[4,16]{1,0:T(4,128)} %bitcast.11, s32[64,128]{1,0:T(8,128)} %bitcast.8, bf16[16,4,8,2048]{3,2,1,0:T(8,128)(2,1)} %frames_hbm.1), custom_call_target="tpu_custom_call" | custom-call | tf_op jit(solution)/shard_map/rocking/pallas_call | solution.py:335
  48.1 2.0 %copy.7 = f32[16,8,8192]{2,1,0:T(8,128)} copy(f32[16,8,8192]{2,1,0:T(8,128)S(1)} %bitcast.7) | data formatting | bytes 8388608

commit v3 on v2

--- a/solution.py
+++ b/solution.py
@@ -93,21 +93,6 @@
     return front + back
 
 
-def sweep(load, emit, low, high, even, odd):
-    before = phi_blur(load(low - 1), even, odd)
-    here = phi_blur(load(low), even, odd)
-    joined = [a + b for a, b in zip(before, here)]
-
-    def step(c, carry):
-        here, joined = carry
-        after = phi_blur(load(c + 1), even, odd)
-        ahead = [a + b for a, b in zip(here, after)]
-        emit(c, [a + b for a, b in zip(joined, ahead)])
-        return after, ahead
-
-    lax.fori_loop(low, high, step, (here, joined), unroll=2)
-
-
 def kernel(
     n_phi,
     rows_ref,
@@ -122,11 +107,13 @@
     staged_ref,
     data_ref,
     estimate_ref,
-    ratio_ref,
+    blurs_ref,
     band_sem,
     frame_sems,
     send_sems,
     recv_sems,
+    last_sends,
+    last_recvs,
     pair_sends,
     pair_recvs,
     local_sems,
@@ -186,30 +173,41 @@
 
     mine = pl.ds(chi * own_phis, own_phis)
 
-    def neighbour_copy(b, number):
-        to_phi, to_chi = peers[number]
+    def neighbour_copy(b, number, tilt, tilts, send_sem, recv_sem, flip):
         back = number < 2
-        from_tilts = pl.ds(0 if back else own_tilts - HALO, HALO)
-        to_tilts = pl.ds(all_tilts - HALO if back else 0, HALO)
-        place = (0 if back else 2) + chi
+        to_chi = lax.rem(flip + number, 2)
+        first = 0 if back else own_tilts - HALO
+        first_there = all_tilts - HALO if back else 0
         return pltpu.make_async_remote_copy(
-            src_ref=staged_ref.at[to_chi, b, from_tilts],
-            dst_ref=data_ref.at[b, to_tilts, mine],
-            send_sem=send_sems.at[b, number],
-            recv_sem=recv_sems.at[b, place],
-            device_id={"chi": to_chi, "phi": to_phi},
+            src_ref=staged_ref.at[to_chi, b, pl.ds(first + tilt, tilts)],
+            dst_ref=data_ref.at[b, pl.ds(first_there + tilt, tilts), mine],
+            send_sem=send_sem,
+            recv_sem=recv_sem,
+            device_id={"chi": to_chi, "phi": before if back else after},
             device_id_type=pl.DeviceIdType.MESH,
         )
 
-    def arrival(b, place):
+    def place_of(number):
+        return (0 if number < 2 else 2) + chi
+
+    def halo_copy(b, number, tilt=0, tilts=HALO):
+        return neighbour_copy(b, number, tilt, tilts, send_sems.at[b, number], recv_sems.at[b, place_of(number)], b)
+
+    def last_copy(number, step):
+        tilt = step if number < 2 else HALO - 1 - step
+        return neighbour_copy(
+            blocks - 1, number, tilt, 1, last_sends.at[number, step], last_recvs.at[place_of(number), step], step
+        )
+
+    def arrival(b, place, tilt, tilts, recv_sem):
         back = place < 2
-        to_tilts = pl.ds(all_tilts - HALO if back else 0, HALO)
         from_chi = place % 2
+        first = all_tilts - HALO if back else 0
         return pltpu.make_async_remote_copy(
-            src_ref=staged_ref.at[0, b, pl.ds(0, HALO)],
-            dst_ref=data_ref.at[b, to_tilts, pl.ds(from_chi * own_phis, own_phis)],
-            send_sem=send_sems.at[b, place],
-            recv_sem=recv_sems.at[b, place],
+            src_ref=staged_ref.at[0, b, pl.ds(0, tilts)],
+            dst_ref=data_ref.at[b, pl.ds(first + tilt, tilts), pl.ds(from_chi * own_phis, own_phis)],
+            send_sem=send_sems.at[0, place],
+            recv_sem=recv_sem,
             device_id={"chi": from_chi, "phi": after if back else before},
             device_id_type=pl.DeviceIdType.MESH,
         )
@@ -230,16 +228,28 @@
         return pltpu.make_async_copy(staged_ref.at[chi, b], data_ref.at[b, middle, mine], local_sems.at[b])
 
     loads[0].wait()
-    shift_tilts(firsts[0], sizes[0])
     loads[1].wait()
-    shift_tilts(firsts[1], sizes[1])
     pl.semaphore_wait(barrier, 1 + 2 * has_before.astype(jnp.int32) + 2 * has_after.astype(jnp.int32))
 
+    def shift_edges(tilt, carry):
+        for first in firsts[:2]:
+            shift_tilt(first + tilt, rows_ref, cols_ref, index_ref, frames_ref, spread_ref, staged_ref)
+        with_neighbours(lambda number: halo_copy(0, number, tilt, 1).start())
+        return carry
+
+    lax.fori_loop(0, HALO, shift_edges, 0)
+
     def send_halos(b, carry):
-        with_neighbours(lambda number: neighbour_copy(b, number).start())
-        return carry
-
-    lax.fori_loop(0, blocks, send_halos, 0)
+        with_neighbours(lambda number: halo_copy(b, number).start())
+        return carry
+
+    lax.fori_loop(1, blocks - 1, send_halos, 0)
+
+    def send_last(step, carry):
+        with_neighbours(lambda number: last_copy(number, step).start())
+        return carry
+
+    lax.fori_loop(0, HALO, send_last, 0)
     loads[2].wait()
     shift_tilts(firsts[2], sizes[2])
 
@@ -254,72 +264,131 @@
     left_add = jnp.where(phi == 0, 0.0, 0.1)
     right_add = jnp.where(phi == n_phi - 1, 0.0, 0.1)
 
-    def block(b, carry):
+    def block(b, last):
+        even, odd = tap_matrices(band_ref[pl.ds(pl.multiple_of(b * SUBS, SUBS), SUBS), :])
+        stages = 2 * ITERS
+
+        def blurs(stage, c):
+            return [blurs_ref[stage, c, p] for p in range(phis)]
+
+        def keep_blur(stage, c, values):
+            made = phi_blur(values, even, odd)
+            for p in range(phis):
+                blurs_ref[stage, c, p] = made[p]
+            return made
+
+        def first_estimate(c, add):
+            return [data_ref[b, c, p] + add for p in range(phis)]
+
+        def finish_cell(stage, c, mixed, add):
+            if stage % 2 == 1:
+                made = [data_ref[b, c, p] / (mixed[p] + 0.1) for p in range(phis)]
+            else:
+                old = first_estimate(c, add) if stage == 2 else [estimate_ref[c, p] for p in range(phis)]
+                made = [o * m for o, m in zip(old, mixed)]
+                if stage < stages:
+                    for p in range(phis):
+                        estimate_ref[c, p] = made[p]
+            if stage < stages:
+                return keep_blur(stage, c, made)
+            planes = pl.ds(pl.multiple_of(b * SUBS, SUBS), SUBS)
+            out_ref[c - HALO, planes] = jnp.swapaxes(jnp.stack(made), 0, 1)
+            return made
+
         pair_copy(b, pl.ds(other * own_phis, own_phis)).wait_recv()
         local_copy(b).wait()
+
+        def start_cell(c, carry):
+            keep_blur(0, c, first_estimate(c, 0.1))
+            return carry
+
+        lax.fori_loop(HALO, HALO + own_tilts, start_cell, 0, unroll=2)
+        for stage in range(1, stages + 1):
+            low, high = HALO + stage, HALO + own_tilts - stage
+
+            def cell(c, carry):
+                here, joined = carry
+                beyond = blurs(stage - 1, c + 1)
+                ahead = [x + y for x, y in zip(here, beyond)]
+                finish_cell(stage, c, [x + y for x, y in zip(joined, ahead)], 0.1)
+                return beyond, ahead
+
+            near, here = blurs(stage - 1, low - 1), blurs(stage - 1, low)
+            lax.fori_loop(low, high, cell, (here, [x + y for x, y in zip(near, here)]), unroll=2)
+
         nothing = jnp.zeros(data_ref.shape[2:], jnp.float32)
-
-        @pl.when(has_before)
-        def _():
-            for place in (2, 3):
-                arrival(b, place).wait_recv()
 
         @pl.when(phi == 0)
         def _():
             for c in range(HALO):
                 data_ref[b, c] = nothing
 
-        @pl.when(has_after)
-        def _():
-            for place in (0, 1):
-                arrival(b, place).wait_recv()
-
         @pl.when(phi == n_phi - 1)
         def _():
             for c in range(all_tilts - HALO, all_tilts):
                 data_ref[b, c] = nothing
 
-        even, odd = tap_matrices(band_ref[pl.ds(pl.multiple_of(b * SUBS, SUBS), SUBS), :])
-
-        def start(c):
-            add = jnp.where(c < HALO, left_add, jnp.where(c >= HALO + own_tilts, right_add, 0.1))
-            return [data_ref[b, c, p] + add for p in range(phis)]
-
-        def held(c):
-            return [estimate_ref[c, p] for p in range(phis)]
-
-        def ratios(c):
-            return [ratio_ref[c, p] for p in range(phis)]
-
-        for iteration in range(ITERS):
-            estimate = start if iteration == 0 else held
-            margin = 2 * iteration + 1
-
-            def to_ratio(c, blurred):
-                for p in range(phis):
-                    ratio_ref[c, p] = data_ref[b, c, p] / (blurred[p] + 0.1)
-
-            def to_estimate(c, factor):
-                made = [a * f for a, f in zip(estimate(c), factor)]
-                if iteration < ITERS - 1:
-                    for p in range(phis):
-                        estimate_ref[c, p] = made[p]
+        def wait_for(places, back_tilt, step):
+            for place in places:
+                if last:
+                    arrival(b, place, back_tilt, 1, last_recvs.at[place, step]).wait_recv()
                 else:
-                    planes = pl.ds(pl.multiple_of(b * SUBS, SUBS), SUBS)
-                    out_ref[c - HALO, planes] = jnp.swapaxes(jnp.stack(made), 0, 1)
-
-            sweep(estimate, to_ratio, margin, all_tilts - margin, even, odd)
-            sweep(ratios, to_estimate, margin + 1, all_tilts - margin - 1, even, odd)
-        return carry
-
-    lax.fori_loop(0, blocks, block, 0)
+                    arrival(b, place, 0, HALO, recv_sems.at[b, place]).wait_recv()
+
+        def wait_step(step):
+            @pl.when(has_before)
+            def _():
+                wait_for((2, 3), HALO - 1 - step, step)
+
+            @pl.when(has_after)
+            def _():
+                wait_for((0, 1), step, step)
+
+        if not last:
+            wait_step(0)
+
+        def wave(step, carry):
+            if last:
+                wait_step(step)
+            tilts = (HALO - 1 - step, HALO + own_tilts + step)
+            steps = (1, -1)
+            adds = (left_add, right_add)
+            chain = [keep_blur(0, c, first_estimate(c, add)) for c, add in zip(tilts, adds)]
+            for stage in range(1, stages + 1):
+                for side in range(2):
+                    c = tilts[side] + steps[side] * stage
+                    here, beyond = blurs(stage - 1, c), blurs(stage - 1, c + steps[side])
+                    mixed = [(x + y) + (y + z) for x, y, z in zip(chain[side], here, beyond)]
+                    outside = c < HALO if side == 0 else c >= HALO + own_tilts
+                    chain[side] = finish_cell(stage, c, mixed, jnp.where(outside, adds[side], 0.1))
+            return carry
+
+        lax.fori_loop(0, HALO, wave, 0)
+
+    def some_block(b, carry):
+        block(b, False)
+        return carry
+
+    lax.fori_loop(0, blocks - 1, some_block, 0)
+    block(blocks - 1, True)
 
     def finish(b, carry):
-        with_neighbours(lambda number: neighbour_copy(b, number).wait_send())
+        with_neighbours(lambda number: halo_copy(b, number).wait_send())
+        return carry
+
+    lax.fori_loop(0, blocks - 1, finish, 0)
+
+    def finish_last(step, carry):
+        with_neighbours(lambda number: last_copy(number, step).wait_send())
+        return carry
+
+    lax.fori_loop(0, HALO, finish_last, 0)
+
+    def finish_pair(b, carry):
         pair_copy(b, mine).wait_send()
         return carry
 
-    lax.fori_loop(0, blocks, finish, 0)
+    lax.fori_loop(0, blocks, finish_pair, 0)
 
 
 def body(n_phi, frames, drift_rows, drift_cols, weight_index, blur_band):
@@ -344,11 +413,13 @@
             pltpu.VMEM((2, blocks, tilts, own_phis) + tile, jnp.float32),
             pltpu.VMEM((blocks, all_tilts, phis) + tile, jnp.float32),
             pltpu.VMEM((all_tilts, phis) + tile, jnp.float32),
-            pltpu.VMEM((all_tilts, phis) + tile, jnp.float32),
+            pltpu.VMEM((2 * ITERS, all_tilts, phis) + tile, jnp.float32),
             pltpu.SemaphoreType.DMA,
             pltpu.SemaphoreType.DMA((3,)),
-            pltpu.SemaphoreType.DMA((blocks, REMOTE)),
-            pltpu.SemaphoreType.DMA((blocks, REMOTE)),
+            pltpu.SemaphoreType.DMA((blocks - 1, REMOTE)),
+            pltpu.SemaphoreType.DMA((blocks - 1, REMOTE)),
+            pltpu.SemaphoreType.DMA((REMOTE, HALO)),
+            pltpu.SemaphoreType.DMA((REMOTE, HALO)),
             pltpu.SemaphoreType.DMA((blocks,)),
             pltpu.SemaphoreType.DMA((blocks,)),
             pltpu.SemaphoreType.DMA((blocks,)),

time: 50.3 us -> 47.1 us (0.936)
  Pallas kernels: 48.1 us -> 45 us
    pallas_call x1, Pallas kernels: 48.1 us -> 45 us  [body(): pl.pallas_call(functools.partial(kernel, n_phi), out_shape=pltpu.VMEM((ti...]
where the time goes in v3:
time: 47.1 us; the launch traced here: 47 us
  Pallas kernels  45 us (96%)
  local copies, waits for them, and re-layouts  2.02 us (4%)
    pallas_call x1, Pallas kernels, body(): pl.pallas_call(functools.partial(kernel, n_phi), out_shape=pltpu.VMEM((ti...  45 us
    unnamed x1, local copies, waits for them, and re-layouts  2.02 us

profile of v3, /device:TPU:97, one launch (start us, length us, event | category | flops | bytes accessed | tf_op | source)
XLA Modules:
  0.0 47.0 jit_solution(3504648888414730508)
XLA Ops:
  0.0 45.0 %rocking.1 = f32[16,64,8,128]{3,2,1,0:T(8,128)S(1)} custom-call(s32[4,16]{1,0:T(4,128)} %bitcast.9, s32[4,16]{1,0:T(4,128)} %bitcast.10, s32[4,16]{1,0:T(4,128)} %bitcast.11, s32[64,128]{1,0:T(8,128)} %bitcast.8, bf16[16,4,8,2048]{3,2,1,0:T(8,128)(2,1)} %frames_hbm.1), custom_call_target="tpu_custom_call" | custom-call | tf_op jit(solution)/shard_map/rocking/pallas_call | solution.py:404
  45.0 2.0 %copy.7 = f32[16,8,8192]{2,1,0:T(8,128)} copy(f32[16,8,8192]{2,1,0:T(8,128)S(1)} %bitcast.7) | data formatting | bytes 8388608

commit v4 on v3

--- a/solution.py
+++ b/solution.py
@@ -46,7 +46,7 @@
             group = jnp.stack(moved[h * SUBS : (h + 1) * SUBS])
             spread_ref[p, PAD_ROWS : PAD_ROWS + rows, h] = jnp.swapaxes(group, 0, 1)
     for p in range(own_phis):
-        drift_row = rows_ref[p, tilt]
+        drift_row = jnp.clip(rows_ref[p, tilt], -MOST_ROWS, MOST_ROWS)
         frac_y = (index_ref[p, tilt] >> 3).astype(jnp.float32) / 8.0
         for r in range(rows):
             row = (1.0 - frac_y) * spread_ref[p, r + PAD_ROWS - drift_row] + frac_y * spread_ref[
@@ -95,12 +95,15 @@
 
 def kernel(
     n_phi,
+    rows_hbm,
+    cols_hbm,
+    index_hbm,
+    band_hbm,
+    frames_hbm,
+    out_ref,
     rows_ref,
     cols_ref,
     index_ref,
-    band_hbm,
-    frames_hbm,
-    out_ref,
     band_ref,
     frames_ref,
     spread_ref,
@@ -108,8 +111,10 @@
     data_ref,
     estimate_ref,
     blurs_ref,
+    table_sems,
     band_sem,
-    frame_sems,
+    edge_sems,
+    middle_sem,
     send_sems,
     recv_sems,
     last_sends,
@@ -125,16 +130,24 @@
     has_before, has_after = phi > 0, phi < n_phi - 1
     own_tilts, own_phis = frames_ref.shape[:2]
     blocks, all_tilts, phis = data_ref.shape[:3]
-    sizes = (HALO, HALO, own_tilts - 2 * HALO)
-    firsts = (0, own_tilts - HALO, HALO)
-
+    firsts = (0, own_tilts - HALO)
+
+    def edge_load(tilt, side):
+        at = firsts[side] + tilt
+        return pltpu.make_async_copy(frames_hbm.at[at], frames_ref.at[at], edge_sems.at[tilt, side])
+
+    tables = ((rows_hbm, rows_ref), (cols_hbm, cols_ref), (index_hbm, index_ref))
+    table_loads = [pltpu.make_async_copy(a, b, table_sems.at[i]) for i, (a, b) in enumerate(tables)]
+    for load in table_loads:
+        load.start()
+    for tilt in range(HALO):
+        for side in range(2):
+            edge_load(tilt, side).start()
+    inner = pl.ds(HALO, own_tilts - 2 * HALO)
+    middle_load = pltpu.make_async_copy(frames_hbm.at[inner], frames_ref.at[inner], middle_sem)
+    middle_load.start()
     band_load = pltpu.make_async_copy(band_hbm, band_ref, band_sem)
     band_load.start()
-    loads = []
-    for number, (first, size) in enumerate(zip(firsts, sizes)):
-        part = pl.ds(first, size)
-        loads.append(pltpu.make_async_copy(frames_hbm.at[part], frames_ref.at[part], frame_sems.at[number]))
-        loads[-1].start()
 
     barrier = pltpu.get_barrier_semaphore()
     peers = [(before, 0), (before, 1), (after, 0), (after, 1)]
@@ -163,13 +176,6 @@
         for r in range(PAD_ROWS):
             spread_ref[p, r] = empty
             spread_ref[p, spread_ref.shape[1] - 1 - r] = empty
-
-    def shift_tilts(first, size):
-        def step(tilt, carry):
-            shift_tilt(tilt, rows_ref, cols_ref, index_ref, frames_ref, spread_ref, staged_ref)
-            return carry
-
-        lax.fori_loop(first, first + size, step, 0)
 
     mine = pl.ds(chi * own_phis, own_phis)
 
@@ -227,13 +233,21 @@
     def local_copy(b):
         return pltpu.make_async_copy(staged_ref.at[chi, b], data_ref.at[b, middle, mine], local_sems.at[b])
 
-    loads[0].wait()
-    loads[1].wait()
-    pl.semaphore_wait(barrier, 1 + 2 * has_before.astype(jnp.int32) + 2 * has_after.astype(jnp.int32))
+    def shift_at(tilt):
+        shift_tilt(tilt, rows_ref, cols_ref, index_ref, frames_ref, spread_ref, staged_ref)
+
+    for load in table_loads:
+        load.wait()
 
     def shift_edges(tilt, carry):
-        for first in firsts[:2]:
-            shift_tilt(first + tilt, rows_ref, cols_ref, index_ref, frames_ref, spread_ref, staged_ref)
+        for side in range(2):
+            edge_load(tilt, side).wait()
+            shift_at(firsts[side] + tilt)
+
+        @pl.when(tilt == 0)
+        def _():
+            pl.semaphore_wait(barrier, 1 + 2 * has_before.astype(jnp.int32) + 2 * has_after.astype(jnp.int32))
+
         with_neighbours(lambda number: halo_copy(0, number, tilt, 1).start())
         return carry
 
@@ -250,8 +264,13 @@
         return carry
 
     lax.fori_loop(0, HALO, send_last, 0)
-    loads[2].wait()
-    shift_tilts(firsts[2], sizes[2])
+    middle_load.wait()
+
+    def shift_inner(tilt, carry):
+        shift_at(tilt)
+        return carry
+
+    lax.fori_loop(HALO, own_tilts - HALO, shift_inner, 0)
 
     def send_pairs(b, carry):
         pair_copy(b, mine).start()
@@ -400,13 +419,16 @@
     tile = (SUBS, LANES)
     all_tilts = tilts + 2 * HALO
     hbm = pl.BlockSpec(memory_space=pltpu.HBM)
-    smem = pl.BlockSpec(memory_space=pltpu.SMEM)
+    table = pltpu.SMEM((own_phis, tilts), jnp.int32)
     out = pl.pallas_call(
         functools.partial(kernel, n_phi),
         out_shape=pltpu.VMEM((tilts, planes, phis, LANES), jnp.float32),
-        in_specs=[smem] * 3 + [hbm] * 2,
+        in_specs=[hbm] * 5,
         out_specs=pl.BlockSpec(memory_space=pltpu.VMEM),
         scratch_shapes=[
+            table,
+            table,
+            table,
             pltpu.VMEM((planes, LANES), jnp.int32),
             pltpu.VMEM(frames.shape, frames.dtype),
             pltpu.VMEM((own_phis, rows + 2 * PAD_ROWS, cols // LANES // SUBS) + tile, jnp.float32),
@@ -414,8 +436,10 @@
             pltpu.VMEM((blocks, all_tilts, phis) + tile, jnp.float32),
             pltpu.VMEM((all_tilts, phis) + tile, jnp.float32),
             pltpu.VMEM((2 * ITERS, all_tilts, phis) + tile, jnp.float32),
+            pltpu.SemaphoreType.DMA((3,)),
             pltpu.SemaphoreType.DMA,
-            pltpu.SemaphoreType.DMA((3,)),
+            pltpu.SemaphoreType.DMA((HALO, 2)),
+            pltpu.SemaphoreType.DMA,
             pltpu.SemaphoreType.DMA((blocks - 1, REMOTE)),
             pltpu.SemaphoreType.DMA((blocks - 1, REMOTE)),
             pltpu.SemaphoreType.DMA((REMOTE, HALO)),

time: 47.1 us -> 45.9 us (0.975)
  Pallas kernels: 45 us -> 43.8 us
    pallas_call x1, Pallas kernels: 45 us -> 43.8 us  [body(): pl.pallas_call(functools.partial(kernel, n_phi), out_shape=pltpu.VMEM((ti...]
where the time goes in v4:
time: 45.9 us; the launch traced here: 45.8 us
  Pallas kernels  43.8 us (95%)
  local copies, waits for them, and re-layouts  2.02 us (4%)
    pallas_call x1, Pallas kernels, body(): pl.pallas_call(functools.partial(kernel, n_phi), out_shape=pltpu.VMEM((ti...  43.8 us
    unnamed x1, local copies, waits for them, and re-layouts  2.02 us

profile of v4, /device:TPU:97, one launch (start us, length us, event | category | flops | bytes accessed | tf_op | source)
XLA Modules:
  0.0 45.8 jit_solution(7179521945452179484)
XLA Ops:
  0.0 43.8 %rocking.1 = f32[16,64,8,128]{3,2,1,0:T(8,128)S(1)} custom-call(s32[4,16]{1,0:T(4,128)} %bitcast.9, s32[4,16]{1,0:T(4,128)} %bitcast.10, s32[4,16]{1,0:T(4,128)} %bitcast.11, s32[64,128]{1,0:T(8,128)} %bitcast.8, bf16[16,4,8,2048]{3,2,1,0:T(8,128)(2,1)} %frames_hbm.1), custom_call_target="tpu_custom_call" | custom-call | tf_op jit(solution)/shard_map/rocking/pallas_call | solution.py:423
  43.8 2.0 %copy.7 = f32[16,8,8192]{2,1,0:T(8,128)} copy(f32[16,8,8192]{2,1,0:T(8,128)S(1)} %bitcast.7) | data formatting | bytes 8388608

commit v5 on v4

--- a/solution.py
+++ b/solution.py
@@ -13,6 +13,10 @@
 SUBS = 8
 MOST_ROWS = 2
 PAD_ROWS = MOST_ROWS + 1
+ROW = 4
+PLANE = 16
+FORWARD_AT = 2
+RELAYS = 2
 REMOTE = 4
 
 
@@ -119,6 +123,10 @@
     recv_sems,
     last_sends,
     last_recvs,
+    relay_ref,
+    relay_sends,
+    relay_recvs,
+    forward_sends,
     pair_sends,
     pair_recvs,
     local_sems,
@@ -128,6 +136,8 @@
     before = lax.rem(phi + n_phi - 1, n_phi)
     after = lax.rem(phi + 1, n_phi)
     has_before, has_after = phi > 0, phi < n_phi - 1
+    spot, plane = lax.rem(phi, PLANE), phi // PLANE
+    planes = n_phi // PLANE
     own_tilts, own_phis = frames_ref.shape[:2]
     blocks, all_tilts, phis = data_ref.shape[:3]
     firsts = (0, own_tilts - HALO)
@@ -141,7 +151,7 @@
     for load in table_loads:
         load.start()
     for tilt in range(HALO):
-        for side in range(2):
+        for side in (1, 0):
             edge_load(tilt, side).start()
     inner = pl.ds(HALO, own_tilts - 2 * HALO)
     middle_load = pltpu.make_async_copy(frames_hbm.at[inner], frames_ref.at[inner], middle_sem)
@@ -168,8 +178,42 @@
             for number in (2, 3):
                 act(number)
 
+    def as_feeder(act):
+        @pl.when(spot == PLANE - 1)
+        def _():
+            pl.when(plane < planes - 1)(act)
+
+    def as_relay(k, act):
+        @pl.when(spot == ROW * k + ROW - 1)
+        def _():
+            pl.when(plane > 0)(act)
+
+    def as_fed(act):
+        @pl.when(spot == 0)
+        def _():
+            pl.when(plane > 0)(act)
+
+    def wrapped(to_phi):
+        return lax.rem(to_phi + n_phi, n_phi)
+
+    def greet_feeder(k):
+        for to_chi in range(2):
+            greet(wrapped(phi - ROW * (k + 1)), to_chi)
+
+    def greet_relays():
+        for k in range(RELAYS):
+            greet(wrapped(phi + ROW * (k + 1) - 1), chi)
+
     with_neighbours(lambda number: greet(*peers[number]))
     greet(phi, other)
+    for k in range(RELAYS):
+        as_relay(k, functools.partial(greet_feeder, k))
+    as_fed(greet_relays)
+    one_plane_up = (plane > 0).astype(jnp.int32)
+    feeding = (spot == PLANE - 1).astype(jnp.int32) * (plane < planes - 1).astype(jnp.int32)
+    relaying = sum((spot == ROW * (k + 1) - 1).astype(jnp.int32) for k in range(RELAYS)) * one_plane_up
+    greetings = 1 + 2 * has_before.astype(jnp.int32) + 2 * has_after.astype(jnp.int32)
+    greetings = greetings + 2 * RELAYS * feeding + relaying
 
     empty = jnp.zeros(spread_ref.shape[2:], jnp.float32)
     for p in range(own_phis):
@@ -240,13 +284,13 @@
         load.wait()
 
     def shift_edges(tilt, carry):
-        for side in range(2):
+        for side in (1, 0):
             edge_load(tilt, side).wait()
             shift_at(firsts[side] + tilt)
 
         @pl.when(tilt == 0)
         def _():
-            pl.semaphore_wait(barrier, 1 + 2 * has_before.astype(jnp.int32) + 2 * has_after.astype(jnp.int32))
+            pl.semaphore_wait(barrier, greetings)
 
         with_neighbours(lambda number: halo_copy(0, number, tilt, 1).start())
         return carry
@@ -259,8 +303,64 @@
 
     lax.fori_loop(1, blocks - 1, send_halos, 0)
 
+    def relay_copy(k, to_chi):
+        return pltpu.make_async_remote_copy(
+            src_ref=staged_ref.at[to_chi, blocks - 1, pl.ds(own_tilts - HALO + k, 1)],
+            dst_ref=relay_ref.at[chi],
+            send_sem=relay_sends.at[k, to_chi],
+            recv_sem=relay_recvs.at[chi],
+            device_id={"chi": to_chi, "phi": wrapped(phi + ROW * (k + 1))},
+            device_id_type=pl.DeviceIdType.MESH,
+        )
+
+    def forward_copy(k, from_chi):
+        return pltpu.make_async_remote_copy(
+            src_ref=relay_ref.at[from_chi],
+            dst_ref=data_ref.at[blocks - 1, pl.ds(k, 1), pl.ds(from_chi * own_phis, own_phis)],
+            send_sem=forward_sends.at[from_chi],
+            recv_sem=last_recvs.at[2 + from_chi, HALO - 1 - k],
+            device_id={"chi": chi, "phi": wrapped(phi - ROW * (k + 1) + 1)},
+            device_id_type=pl.DeviceIdType.MESH,
+        )
+
+    def relay_arrival(from_chi):
+        return pltpu.make_async_remote_copy(
+            src_ref=staged_ref.at[0, 0, pl.ds(0, 1)],
+            dst_ref=relay_ref.at[from_chi],
+            send_sem=relay_sends.at[0, from_chi],
+            recv_sem=relay_recvs.at[from_chi],
+            device_id={"chi": from_chi, "phi": wrapped(phi - ROW)},
+            device_id_type=pl.DeviceIdType.MESH,
+        )
+
+    def each_relay_copy(act):
+        for k in range(RELAYS):
+            for to_chi in range(2):
+                act(relay_copy(k, to_chi))
+
+    def forward(k):
+        for from_chi in range(2):
+            relay_arrival(from_chi).wait_recv()
+            forward_copy(k, from_chi).start()
+
+    as_feeder(lambda: each_relay_copy(lambda copy: copy.start()))
+    direct = HALO - RELAYS * feeding
+
+    def with_last(step, act):
+        @pl.when(has_before)
+        def _():
+            for number in (0, 1):
+                act(number)
+
+        @pl.when(has_after)
+        def _():
+            @pl.when(step < direct)
+            def _():
+                for number in (2, 3):
+                    act(number)
+
     def send_last(step, carry):
-        with_neighbours(lambda number: last_copy(number, step).start())
+        with_last(step, lambda number: last_copy(number, step).start())
         return carry
 
     lax.fori_loop(0, HALO, send_last, 0)
@@ -310,8 +410,8 @@
                         estimate_ref[c, p] = made[p]
             if stage < stages:
                 return keep_blur(stage, c, made)
-            planes = pl.ds(pl.multiple_of(b * SUBS, SUBS), SUBS)
-            out_ref[c - HALO, planes] = jnp.swapaxes(jnp.stack(made), 0, 1)
+            rows_at = pl.ds(pl.multiple_of(b * SUBS, SUBS), SUBS)
+            out_ref[c - HALO, rows_at] = jnp.swapaxes(jnp.stack(made), 0, 1)
             return made
 
         pair_copy(b, pl.ds(other * own_phis, own_phis)).wait_recv()
@@ -385,6 +485,11 @@
         lax.fori_loop(0, HALO, wave, 0)
 
     def some_block(b, carry):
+        @pl.when(b == FORWARD_AT)
+        def _():
+            for k in range(RELAYS):
+                as_relay(k, functools.partial(forward, k))
+
         block(b, False)
         return carry
 
@@ -398,10 +503,18 @@
     lax.fori_loop(0, blocks - 1, finish, 0)
 
     def finish_last(step, carry):
-        with_neighbours(lambda number: last_copy(number, step).wait_send())
+        with_last(step, lambda number: last_copy(number, step).wait_send())
         return carry
 
     lax.fori_loop(0, HALO, finish_last, 0)
+    as_feeder(lambda: each_relay_copy(lambda copy: copy.wait_send()))
+
+    def finish_forward(k):
+        for from_chi in range(2):
+            forward_copy(k, from_chi).wait_send()
+
+    for k in range(RELAYS):
+        as_relay(k, functools.partial(finish_forward, k))
 
     def finish_pair(b, carry):
         pair_copy(b, mine).wait_send()
@@ -444,6 +557,10 @@
             pltpu.SemaphoreType.DMA((blocks - 1, REMOTE)),
             pltpu.SemaphoreType.DMA((REMOTE, HALO)),
             pltpu.SemaphoreType.DMA((REMOTE, HALO)),
+            pltpu.VMEM((2, 1, own_phis) + tile, jnp.float32),
+            pltpu.SemaphoreType.DMA((RELAYS, 2)),
+            pltpu.SemaphoreType.DMA((2,)),
+            pltpu.SemaphoreType.DMA((2,)),
             pltpu.SemaphoreType.DMA((blocks,)),
             pltpu.SemaphoreType.DMA((blocks,)),
             pltpu.SemaphoreType.DMA((blocks,)),

time: 45.9 us -> 62.9 us (1.37)
  the two profiles are of different devices: /device:TPU:97 before, /device:TPU:111 now
where the time goes in v5:
time: 62.9 us; the launch traced here: 62.8 us
  Pallas kernels  60.8 us (97%)
  local copies, waits for them, and re-layouts  2.02 us (3%)
    pallas_call x1, Pallas kernels, body(): pl.pallas_call(functools.partial(kernel, n_phi), out_shape=pltpu.VMEM((ti...  60.8 us
    unnamed x1, local copies, waits for them, and re-layouts  2.02 us

profile of v5, /device:TPU:111, one launch (start us, length us, event | category | flops | bytes accessed | tf_op | source)
XLA Modules:
  0.0 62.8 jit_solution(3487424234064781797)
XLA Ops:
  0.0 60.8 %rocking.1 = f32[16,64,8,128]{3,2,1,0:T(8,128)S(1)} custom-call(s32[4,16]{1,0:T(4,128)} %bitcast.9, s32[4,16]{1,0:T(4,128)} %bitcast.10, s32[4,16]{1,0:T(4,128)} %bitcast.11, s32[64,128]{1,0:T(8,128)} %bitcast.8, bf16[16,4,8,2048]{3,2,1,0:T(8,128)(2,1)} %frames_hbm.1), custom_call_target="tpu_custom_call" | custom-call | tf_op jit(solution)/shard_map/rocking/pallas_call | solution.py:536
  60.8 2.0 %copy.7 = f32[16,8,8192]{2,1,0:T(8,128)} copy(f32[16,8,8192]{2,1,0:T(8,128)S(1)} %bitcast.7) | data formatting | bytes 8388608

commit v6 on v4

--- a/solution.py
+++ b/solution.py
@@ -8,7 +8,8 @@
 from jax.sharding import PartitionSpec as P
 
 ITERS = 3
-HALO = 2 * ITERS
+STAGES = 2 * ITERS
+HALO = STAGES
 LANES = 128
 SUBS = 8
 MOST_ROWS = 2
@@ -93,6 +94,81 @@
     return front + back
 
 
+def cells(data_ref, estimate_ref, blurs_ref, even, odd, emit):
+    phis = data_ref.shape[1]
+
+    def blurs(stage, c):
+        return [blurs_ref[stage, c, p] for p in range(phis)]
+
+    def keep_blur(stage, c, values, keep=True):
+        made = phi_blur(values, even, odd)
+        if keep:
+            for p in range(phis):
+                blurs_ref[stage, c, p] = made[p]
+        return made
+
+    def first_estimate(c, add):
+        return [data_ref[c, p] + add for p in range(phis)]
+
+    def finish_cell(stage, c, mixed, add, keep=True):
+        if stage % 2 == 1:
+            made = [data_ref[c, p] / (mixed[p] + 0.1) for p in range(phis)]
+        else:
+            old = first_estimate(c, add) if stage == 2 else [estimate_ref[c, p] for p in range(phis)]
+            made = [o * m for o, m in zip(old, mixed)]
+            if stage < STAGES and keep:
+                for p in range(phis):
+                    estimate_ref[c, p] = made[p]
+        if stage < STAGES:
+            return keep_blur(stage, c, made, keep)
+        emit(c, jnp.swapaxes(jnp.stack(made), 0, 1))
+        return made
+
+    return blurs, keep_blur, first_estimate, finish_cell
+
+
+def run_wave(step, own_tilts, adds, helpers, keep=True):
+    blurs, keep_blur, first_estimate, finish_cell = helpers
+    tilts = (HALO - 1 - step, HALO + own_tilts + step)
+    steps = (1, -1)
+    chain = [keep_blur(0, c, first_estimate(c, add), keep) for c, add in zip(tilts, adds)]
+    for stage in range(1, STAGES + 1):
+        for side in range(2):
+            c = tilts[side] + steps[side] * stage
+            here, beyond = blurs(stage - 1, c), blurs(stage - 1, c + steps[side])
+            mixed = [(x + y) + (y + z) for x, y, z in zip(chain[side], here, beyond)]
+            outside = c < HALO if side == 0 else c >= HALO + own_tilts
+            chain[side] = finish_cell(stage, c, mixed, jnp.where(outside, adds[side], 0.1), keep)
+
+
+def end_adds(n_phi):
+    phi = lax.axis_index("phi")
+    return jnp.where(phi == 0, 0.0, 0.1), jnp.where(phi == n_phi - 1, 0.0, 0.1)
+
+
+def deliver(n_phi, source_ref, data_ref, estimate_ref, blurs_ref, band_ref, out_hbm, edge_ref, sems, edge_sems):
+    tilts, planes = source_ref.shape[:2]
+    blocks = planes // SUBS
+    copies = []
+    for t in range(tilts):
+        part = pl.ds(0, planes - SUBS if t in (0, tilts - 1) else planes)
+        copies.append(pltpu.make_async_copy(source_ref.at[t, part], out_hbm.at[t, part], sems.at[t]))
+        copies[-1].start()
+
+    def emit(c, made):
+        edge_ref[0 if c == HALO else 1] = made
+
+    even, odd = tap_matrices(band_ref[...])
+    helpers = cells(data_ref.at[blocks - 1], estimate_ref, blurs_ref, even, odd, emit)
+    run_wave(HALO - 1, tilts, end_adds(n_phi), helpers, keep=False)
+    for side, t in enumerate((0, tilts - 1)):
+        part = pl.ds(planes - SUBS, SUBS)
+        copies.append(pltpu.make_async_copy(edge_ref.at[side], out_hbm.at[t, part], edge_sems.at[side]))
+        copies[-1].start()
+    for copy in copies:
+        copy.wait()
+
+
 def kernel(
     n_phi,
     rows_hbm,
@@ -101,6 +177,10 @@
     band_hbm,
     frames_hbm,
     out_ref,
+    data_ref,
+    estimate_ref,
+    blurs_ref,
+    last_band_ref,
     rows_ref,
     cols_ref,
     index_ref,
@@ -108,9 +188,6 @@
     frames_ref,
     spread_ref,
     staged_ref,
-    data_ref,
-    estimate_ref,
-    blurs_ref,
     table_sems,
     band_sem,
     edge_sems,
@@ -136,40 +213,39 @@
         at = firsts[side] + tilt
         return pltpu.make_async_copy(frames_hbm.at[at], frames_ref.at[at], edge_sems.at[tilt, side])
 
+    barrier = pltpu.get_barrier_semaphore()
+    peers = [(before, 0), (before, 1), (after, 0), (after, 1)]
+
+    def greet(to_phi, to_chi):
+        pl.semaphore_signal(
+            barrier, inc=1, device_id={"chi": to_chi, "phi": to_phi}, device_id_type=pl.DeviceIdType.MESH
+        )
+
+    def with_neighbours(act):
+        for numbers in ((0, 2), (1, 3)):
+            @pl.when(has_before)
+            def _():
+                act(numbers[0])
+
+            @pl.when(has_after)
+            def _():
+                act(numbers[1])
+
+    with_neighbours(lambda number: greet(*peers[number]))
+    greet(phi, other)
+
     tables = ((rows_hbm, rows_ref), (cols_hbm, cols_ref), (index_hbm, index_ref))
     table_loads = [pltpu.make_async_copy(a, b, table_sems.at[i]) for i, (a, b) in enumerate(tables)]
     for load in table_loads:
         load.start()
     for tilt in range(HALO):
-        for side in range(2):
+        for side in (1, 0):
             edge_load(tilt, side).start()
     inner = pl.ds(HALO, own_tilts - 2 * HALO)
     middle_load = pltpu.make_async_copy(frames_hbm.at[inner], frames_ref.at[inner], middle_sem)
     middle_load.start()
     band_load = pltpu.make_async_copy(band_hbm, band_ref, band_sem)
     band_load.start()
-
-    barrier = pltpu.get_barrier_semaphore()
-    peers = [(before, 0), (before, 1), (after, 0), (after, 1)]
-
-    def greet(to_phi, to_chi):
-        pl.semaphore_signal(
-            barrier, inc=1, device_id={"chi": to_chi, "phi": to_phi}, device_id_type=pl.DeviceIdType.MESH
-        )
-
-    def with_neighbours(act):
-        @pl.when(has_before)
-        def _():
-            for number in (0, 1):
-                act(number)
-
-        @pl.when(has_after)
-        def _():
-            for number in (2, 3):
-                act(number)
-
-    with_neighbours(lambda number: greet(*peers[number]))
-    greet(phi, other)
 
     empty = jnp.zeros(spread_ref.shape[2:], jnp.float32)
     for p in range(own_phis):
@@ -240,7 +316,7 @@
         load.wait()
 
     def shift_edges(tilt, carry):
-        for side in range(2):
+        for side in (1, 0):
             edge_load(tilt, side).wait()
             shift_at(firsts[side] + tilt)
 
@@ -280,39 +356,18 @@
     lax.fori_loop(0, blocks, send_pairs, 0)
     band_load.wait()
 
-    left_add = jnp.where(phi == 0, 0.0, 0.1)
-    right_add = jnp.where(phi == n_phi - 1, 0.0, 0.1)
+    adds = end_adds(n_phi)
 
     def block(b, last):
         even, odd = tap_matrices(band_ref[pl.ds(pl.multiple_of(b * SUBS, SUBS), SUBS), :])
-        stages = 2 * ITERS
-
-        def blurs(stage, c):
-            return [blurs_ref[stage, c, p] for p in range(phis)]
-
-        def keep_blur(stage, c, values):
-            made = phi_blur(values, even, odd)
-            for p in range(phis):
-                blurs_ref[stage, c, p] = made[p]
-            return made
-
-        def first_estimate(c, add):
-            return [data_ref[b, c, p] + add for p in range(phis)]
-
-        def finish_cell(stage, c, mixed, add):
-            if stage % 2 == 1:
-                made = [data_ref[b, c, p] / (mixed[p] + 0.1) for p in range(phis)]
-            else:
-                old = first_estimate(c, add) if stage == 2 else [estimate_ref[c, p] for p in range(phis)]
-                made = [o * m for o, m in zip(old, mixed)]
-                if stage < stages:
-                    for p in range(phis):
-                        estimate_ref[c, p] = made[p]
-            if stage < stages:
-                return keep_blur(stage, c, made)
-            planes = pl.ds(pl.multiple_of(b * SUBS, SUBS), SUBS)
-            out_ref[c - HALO, planes] = jnp.swapaxes(jnp.stack(made), 0, 1)
-            return made
+        rows_at = pl.ds(pl.multiple_of(b * SUBS, SUBS), SUBS)
+
+        def emit(c, made):
+            out_ref[c - HALO, rows_at] = made
+
+        blurs, keep_blur, first_estimate, finish_cell = cells(
+            data_ref.at[b], estimate_ref, blurs_ref, even, odd, emit
+        )
 
         pair_copy(b, pl.ds(other * own_phis, own_phis)).wait_recv()
         local_copy(b).wait()
@@ -322,7 +377,7 @@
             return carry
 
         lax.fori_loop(HALO, HALO + own_tilts, start_cell, 0, unroll=2)
-        for stage in range(1, stages + 1):
+        for stage in range(1, STAGES + 1):
             low, high = HALO + stage, HALO + own_tilts - stage
 
             def cell(c, carry):
@@ -366,23 +421,18 @@
         if not last:
             wait_step(0)
 
+        helpers = blurs, keep_blur, first_estimate, finish_cell
+
         def wave(step, carry):
             if last:
                 wait_step(step)
-            tilts = (HALO - 1 - step, HALO + own_tilts + step)
-            steps = (1, -1)
-            adds = (left_add, right_add)
-            chain = [keep_blur(0, c, first_estimate(c, add)) for c, add in zip(tilts, adds)]
-            for stage in range(1, stages + 1):
-                for side in range(2):
-                    c = tilts[side] + steps[side] * stage
-                    here, beyond = blurs(stage - 1, c), blurs(stage - 1, c + steps[side])
-                    mixed = [(x + y) + (y + z) for x, y, z in zip(chain[side], here, beyond)]
-                    outside = c < HALO if side == 0 else c >= HALO + own_tilts
-                    chain[side] = finish_cell(stage, c, mixed, jnp.where(outside, adds[side], 0.1))
+            run_wave(step, own_tilts, adds, helpers)
             return carry
 
-        lax.fori_loop(0, HALO, wave, 0)
+        lax.fori_loop(0, HALO - 1 if last else HALO, wave, 0)
+        if last:
+            last_band_ref[...] = band_ref[rows_at, :]
+            wait_step(HALO - 1)
 
     def some_block(b, carry):
         block(b, False)
@@ -420,11 +470,18 @@
     all_tilts = tilts + 2 * HALO
     hbm = pl.BlockSpec(memory_space=pltpu.HBM)
     table = pltpu.SMEM((own_phis, tilts), jnp.int32)
-    out = pl.pallas_call(
+    vmem = pl.BlockSpec(memory_space=pltpu.VMEM)
+    held = pl.pallas_call(
         functools.partial(kernel, n_phi),
-        out_shape=pltpu.VMEM((tilts, planes, phis, LANES), jnp.float32),
+        out_shape=(
+            pltpu.VMEM((tilts, planes, phis, LANES), jnp.float32),
+            pltpu.VMEM((blocks, all_tilts, phis) + tile, jnp.float32),
+            pltpu.VMEM((all_tilts, phis) + tile, jnp.float32),
+            pltpu.VMEM((STAGES, all_tilts, phis) + tile, jnp.float32),
+            pltpu.VMEM(tile, jnp.int32),
+        ),
         in_specs=[hbm] * 5,
-        out_specs=pl.BlockSpec(memory_space=pltpu.VMEM),
+        out_specs=(vmem,) * 5,
         scratch_shapes=[
             table,
             table,
@@ -433,9 +490,6 @@
             pltpu.VMEM(frames.shape, frames.dtype),
             pltpu.VMEM((own_phis, rows + 2 * PAD_ROWS, cols // LANES // SUBS) + tile, jnp.float32),
             pltpu.VMEM((2, blocks, tilts, own_phis) + tile, jnp.float32),
-            pltpu.VMEM((blocks, all_tilts, phis) + tile, jnp.float32),
-            pltpu.VMEM((all_tilts, phis) + tile, jnp.float32),
-            pltpu.VMEM((2 * ITERS, all_tilts, phis) + tile, jnp.float32),
             pltpu.SemaphoreType.DMA((3,)),
             pltpu.SemaphoreType.DMA,
             pltpu.SemaphoreType.DMA((HALO, 2)),
@@ -449,10 +503,24 @@
             pltpu.SemaphoreType.DMA((blocks,)),
         ],
         compiler_params=pltpu.CompilerParams(
-            collective_id=0, has_side_effects=True, vmem_limit_bytes=56 * 1024 * 1024
+            collective_id=0, has_side_effects=True, vmem_limit_bytes=45 * 1024 * 1024
         ),
         name="rocking",
     )(drift_rows.T, drift_cols.T, weight_index.T, blur_band.reshape(planes, LANES), frames)
+    held = [pltpu.with_memory_space_constraint(part, pltpu.VMEM) for part in held]
+    out = pl.pallas_call(
+        functools.partial(deliver, n_phi),
+        out_shape=jax.ShapeDtypeStruct((tilts, planes, phis, LANES), jnp.float32),
+        in_specs=[vmem] * 5,
+        out_specs=hbm,
+        scratch_shapes=[
+            pltpu.VMEM((2, SUBS, phis, LANES), jnp.float32),
+            pltpu.SemaphoreType.DMA((tilts,)),
+            pltpu.SemaphoreType.DMA((2,)),
+        ],
+        compiler_params=pltpu.CompilerParams(vmem_limit_bytes=16 * 1024 * 1024),
+        name="deliver",
+    )(*held)
     return out.transpose(0, 2, 1, 3).reshape(tilts, phis, pixels)
 
 

time: 45.9 us -> 45.7 us (level)
  local copies, waits for them, and re-layouts: 2.02 us -> 0 us
  Pallas kernels: 43.8 us -> 45.6 us
    unnamed x1 -> x0, local copies, waits for them, and re-layouts: 2.02 us -> none
    pallas_call x1 -> x2, Pallas kernels: 43.8 us -> 45.6 us  [the longest x1 43.5 us: body(): pl.pallas_call(functools.partial(kernel, n_phi), out_shape=(pltpu.VMEM((t...]
where the time goes in v6:
time: 45.7 us; the launch traced here: 45.6 us
  Pallas kernels  45.6 us (100%)
    pallas_call x1, Pallas kernels, body(): pl.pallas_call(functools.partial(kernel, n_phi), out_shape=(pltpu.VMEM((t...  43.5 us
    pallas_call x1, Pallas kernels, body(): pl.pallas_call(functools.partial(deliver, n_phi), out_shape=jax.ShapeDtyp...  2.14 us

profile of v6, /device:TPU:97, one launch (start us, length us, event | category | flops | bytes accessed | tf_op | source)
XLA Modules:
  0.0 45.6 jit_solution(14422914722141549719)
XLA Ops:
  0.0 43.5 %rocking.1 = (f32[16,64,8,128]{3,2,1,0:T(8,128)S(1)}, f32[8,28,8,8,128]{4,3,2,1,0:T(8,128)S(1)}, f32[28,8,8,128]{3,2,1,0:T(8,128)S(1)}, f32[6,28,8,8,128]{4,3,2,1,0:T(8,128)S(1)}, s32[8,128]{1,0:T(8,128)S(1)}) custom-call(s32[4,16]{1,0:T(4,128)} %bitcast.8, s32[4,16]{1,0:T(4,128)} %bitcast.9, s32[4,16]{1,0:T(4,128)} %bitcast.10, s32[64,128]{1,0:T(8,128)} %bitcast.7, ...), custom_call_target="tpu_custom_call" | custom-call | tf_op jit(solution)/shard_map/rocking/pallas_call | solution.py:474
  43.5 2.1 %deliver.1 = f32[16,64,8,128]{3,2,1,0:T(8,128)} custom-call(f32[16,64,8,128]{3,2,1,0:T(8,128)S(1)} %get-tuple-element.10.source_ref, f32[8,28,8,8,128]{4,3,2,1,0:T(8,128)S(1)} %get-tuple-element.11.data_ref, f32[28,8,8,128]{3,2,1,0:T(8,128)S(1)} %get-tuple-element.12.estimate_ref, f32[6,28,8,8,128]{4,3,2,1,0:T(8,128)S(1)} %get-tuple-element.13.blurs_ref, ...), custom_call_target="tpu_custom_call" | custom-call | tf_op jit(solution)/shard_map/deliver/pallas_call | solution.py:511

commit v7 on v6

--- a/solution.py
+++ b/solution.py
@@ -14,6 +14,8 @@
 SUBS = 8
 MOST_ROWS = 2
 PAD_ROWS = MOST_ROWS + 1
+PLANE = 16
+EARLY = 3
 REMOTE = 4
 
 
@@ -150,9 +152,11 @@
     tilts, planes = source_ref.shape[:2]
     blocks = planes // SUBS
     copies = []
-    for t in range(tilts):
-        part = pl.ds(0, planes - SUBS if t in (0, tilts - 1) else planes)
-        copies.append(pltpu.make_async_copy(source_ref.at[t, part], out_hbm.at[t, part], sems.at[t]))
+    for number, (first, size, rows) in enumerate(
+        ((1, tilts - 2, planes), (0, 1, planes - SUBS), (tilts - 1, 1, planes - SUBS))
+    ):
+        at = pl.ds(first, size), pl.ds(0, rows)
+        copies.append(pltpu.make_async_copy(source_ref.at[at], out_hbm.at[at], sems.at[number]))
         copies[-1].start()
 
     def emit(c, made):
@@ -199,6 +203,7 @@
     pair_sends,
     pair_recvs,
     local_sems,
+    far_sem,
 ):
     chi, phi = lax.axis_index("chi"), lax.axis_index("phi")
     other = 1 - chi
@@ -231,8 +236,25 @@
             def _():
                 act(numbers[1])
 
-    with_neighbours(lambda number: greet(*peers[number]))
+    first_chip = (lax.rem(phi, PLANE) == 0).astype(jnp.int32) * has_before.astype(jnp.int32)
+    last_chip = (lax.rem(phi, PLANE) == PLANE - 1).astype(jnp.int32)
+    told_later = first_chip * (1 - chi)
+
+    @pl.when(has_before)
+    def _():
+        greet(before, 0)
+        greet(before, 1)
+
+    @pl.when(has_after)
+    def _():
+        @pl.when(last_chip == 0)
+        def _():
+            greet(after, 0)
+
+        greet(after, 1)
+
     greet(phi, other)
+    greetings = 1 + 2 * (has_before.astype(jnp.int32) - told_later) + 2 * has_after.astype(jnp.int32)
 
     tables = ((rows_hbm, rows_ref), (cols_hbm, cols_ref), (index_hbm, index_ref))
     table_loads = [pltpu.make_async_copy(a, b, table_sems.at[i]) for i, (a, b) in enumerate(tables)]
@@ -315,16 +337,40 @@
     for load in table_loads:
         load.wait()
 
+    def to_before(act, also):
+        @pl.when(has_before)
+        def _():
+            @pl.when(also)
+            def _():
+                act(0)
+                act(1)
+
+    def to_after(act):
+        @pl.when(has_after)
+        def _():
+            act(2)
+            act(3)
+
+    def shift_edge(tilt, side):
+        edge_load(tilt, side).wait()
+        shift_at(firsts[side] + tilt)
+
     def shift_edges(tilt, carry):
-        for side in (1, 0):
-            edge_load(tilt, side).wait()
-            shift_at(firsts[side] + tilt)
+        shift_edge(tilt, 1)
 
         @pl.when(tilt == 0)
         def _():
-            pl.semaphore_wait(barrier, 1 + 2 * has_before.astype(jnp.int32) + 2 * has_after.astype(jnp.int32))
-
-        with_neighbours(lambda number: halo_copy(0, number, tilt, 1).start())
+            pl.semaphore_wait(barrier, greetings)
+
+            @pl.when(first_chip * chi == 1)
+            def _():
+                pl.semaphore_signal(
+                    far_sem, inc=1, device_id={"chi": other, "phi": phi}, device_id_type=pl.DeviceIdType.MESH
+                )
+
+        to_after(lambda number: halo_copy(0, number, tilt, 1).start())
+        shift_edge(tilt, 0)
+        to_before(lambda number: halo_copy(0, number, tilt, 1).start(), told_later == 0)
         return carry
 
     lax.fori_loop(0, HALO, shift_edges, 0)
@@ -333,7 +379,25 @@
         with_neighbours(lambda number: halo_copy(b, number).start())
         return carry
 
-    lax.fori_loop(1, blocks - 1, send_halos, 0)
+    def send_after(b, carry):
+        to_after(lambda number: halo_copy(b, number).start())
+        return carry
+
+    def send_before(b, carry):
+        to_before(lambda number: halo_copy(b, number).start(), True)
+        return carry
+
+    @pl.when(told_later == 0)
+    def _():
+        lax.fori_loop(1, EARLY, send_halos, 0)
+
+    @pl.when(told_later == 1)
+    def _():
+        lax.fori_loop(1, EARLY, send_after, 0)
+        pl.semaphore_wait(far_sem, 1)
+        lax.fori_loop(0, EARLY, send_before, 0)
+
+    lax.fori_loop(EARLY, blocks - 1, send_halos, 0)
 
     def send_last(step, carry):
         with_neighbours(lambda number: last_copy(number, step).start())
@@ -501,6 +565,7 @@
             pltpu.SemaphoreType.DMA((blocks,)),
             pltpu.SemaphoreType.DMA((blocks,)),
             pltpu.SemaphoreType.DMA((blocks,)),
+            pltpu.SemaphoreType.REGULAR,
         ],
         compiler_params=pltpu.CompilerParams(
             collective_id=0, has_side_effects=True, vmem_limit_bytes=45 * 1024 * 1024
@@ -515,7 +580,7 @@
         out_specs=hbm,
         scratch_shapes=[
             pltpu.VMEM((2, SUBS, phis, LANES), jnp.float32),
-            pltpu.SemaphoreType.DMA((tilts,)),
+            pltpu.SemaphoreType.DMA((3,)),
             pltpu.SemaphoreType.DMA((2,)),
         ],
         compiler_params=pltpu.CompilerParams(vmem_limit_bytes=16 * 1024 * 1024),

time: 45.7 us -> 45.7 us (level)
  no operation moved by 1% of the time
where the time goes in v7:
time: 45.7 us; the launch traced here: 45.4 us
  Pallas kernels  45.4 us (99%)
    pallas_call x1, Pallas kernels, body(): pl.pallas_call(functools.partial(kernel, n_phi), out_shape=(pltpu.VMEM((t...  43.3 us
    pallas_call x1, Pallas kernels, body(): pl.pallas_call(functools.partial(deliver, n_phi), out_shape=jax.ShapeDtyp...  2.03 us

profile of v7, /device:TPU:97, one launch (start us, length us, event | category | flops | bytes accessed | tf_op | source)
XLA Modules:
  0.0 45.4 jit_solution(15792904387037873848)
XLA Ops:
  0.0 43.3 %rocking.1 = (f32[16,64,8,128]{3,2,1,0:T(8,128)S(1)}, f32[8,28,8,8,128]{4,3,2,1,0:T(8,128)S(1)}, f32[28,8,8,128]{3,2,1,0:T(8,128)S(1)}, f32[6,28,8,8,128]{4,3,2,1,0:T(8,128)S(1)}, s32[8,128]{1,0:T(8,128)S(1)}) custom-call(s32[4,16]{1,0:T(4,128)} %bitcast.8, s32[4,16]{1,0:T(4,128)} %bitcast.9, s32[4,16]{1,0:T(4,128)} %bitcast.10, s32[64,128]{1,0:T(8,128)} %bitcast.7, ...), custom_call_target="tpu_custom_call" | custom-call | tf_op jit(solution)/shard_map/rocking/pallas_call | solution.py:538
  43.3 2.0 %deliver.1 = f32[16,64,8,128]{3,2,1,0:T(8,128)} custom-call(f32[16,64,8,128]{3,2,1,0:T(8,128)S(1)} %get-tuple-element.10.source_ref, f32[8,28,8,8,128]{4,3,2,1,0:T(8,128)S(1)} %get-tuple-element.11.data_ref, f32[28,8,8,128]{3,2,1,0:T(8,128)S(1)} %get-tuple-element.12.estimate_ref, f32[6,28,8,8,128]{4,3,2,1,0:T(8,128)S(1)} %get-tuple-element.13.blurs_ref, ...), custom_call_target="tpu_custom_call" | custom-call | tf_op jit(solution)/shard_map/deliver/pallas_call | solution.py:576

commit v8 on v7

--- a/solution.py
+++ b/solution.py
@@ -15,7 +15,7 @@
 MOST_ROWS = 2
 PAD_ROWS = MOST_ROWS + 1
 PLANE = 16
-EARLY = 3
+EARLY = 1
 REMOTE = 4
 
 

time: 45.7 us -> 45.7 us (level)
  no operation moved by 1% of the time
where the time goes in v8:
time: 45.7 us; the launch traced here: 45.4 us
  Pallas kernels  45.4 us (99%)
    pallas_call x1, Pallas kernels, body(): pl.pallas_call(functools.partial(kernel, n_phi), out_shape=(pltpu.VMEM((t...  43.3 us
    pallas_call x1, Pallas kernels, body(): pl.pallas_call(functools.partial(deliver, n_phi), out_shape=jax.ShapeDtyp...  2.03 us

profile of v8, /device:TPU:97, one launch (start us, length us, event | category | flops | bytes accessed | tf_op | source)
XLA Modules:
  0.0 45.4 jit_solution(3266777264618174677)
XLA Ops:
  0.0 43.3 %rocking.1 = (f32[16,64,8,128]{3,2,1,0:T(8,128)S(1)}, f32[8,28,8,8,128]{4,3,2,1,0:T(8,128)S(1)}, f32[28,8,8,128]{3,2,1,0:T(8,128)S(1)}, f32[6,28,8,8,128]{4,3,2,1,0:T(8,128)S(1)}, s32[8,128]{1,0:T(8,128)S(1)}) custom-call(s32[4,16]{1,0:T(4,128)} %bitcast.8, s32[4,16]{1,0:T(4,128)} %bitcast.9, s32[4,16]{1,0:T(4,128)} %bitcast.10, s32[64,128]{1,0:T(8,128)} %bitcast.7, ...), custom_call_target="tpu_custom_call" | custom-call | tf_op jit(solution)/shard_map/rocking/pallas_call | solution.py:538
  43.3 2.0 %deliver.1 = f32[16,64,8,128]{3,2,1,0:T(8,128)} custom-call(f32[16,64,8,128]{3,2,1,0:T(8,128)S(1)} %get-tuple-element.10.source_ref, f32[8,28,8,8,128]{4,3,2,1,0:T(8,128)S(1)} %get-tuple-element.11.data_ref, f32[28,8,8,128]{3,2,1,0:T(8,128)S(1)} %get-tuple-element.12.estimate_ref, f32[6,28,8,8,128]{4,3,2,1,0:T(8,128)S(1)} %get-tuple-element.13.blurs_ref, ...), custom_call_target="tpu_custom_call" | custom-call | tf_op jit(solution)/shard_map/deliver/pallas_call | solution.py:576
